TPU v7x, 512 devices: a whole 4x8x8 slice. The times are simulated.
512 devices in a mesh: dp: 8 (over y), tensor: 4 (over z_hi, core), expert: 16 (over x, z_lo).
Axes of the slice: x: 4, y: 8, z: 8 (z_hi: 2, z_lo: 4; z = z_hi * 4 + z_lo), core: 2. Of those that a mesh axis runs over, the one named last changes fastest.
Arguments:
- tokens: bfloat16 [4096, 2048], P('dp', 'tensor'), may hold values from -6 to 6
- grad_out: bfloat16 [4096, 2048], P('dp', 'tensor'), may hold values from -6 to 6
- routes: int32 [4096, 8], P('dp'), may hold values from 0 to 127, all different within a row; in each aligned block of 512 rows (0 to 511, 512 to 1023, ...) at most 48 rows name the same one
- gates: float32 [4096, 8], P('dp'), may hold values from 0.03 to 0.3
- gate_weight: bfloat16 [64, 1536, 2048], P(('expert', 'tensor'), 'dp'), may hold values from -0.125 to 0.125
- up_weight: bfloat16 [64, 1536, 2048], P(('expert', 'tensor'), 'dp'), may hold values from -0.125 to 0.125
- down_weight: bfloat16 [64, 1536, 2048], P(('expert', 'tensor'), 'dp'), may hold values from -0.15625 to 0.15625
Outputs:
- mixed: bfloat16 [4096, 2048], P('dp', 'tensor')
- grad_tokens: bfloat16 [4096, 2048], P('dp', 'tensor')
- grad_gates: float32 [4096, 8], P('dp')
Inputs may be any that keep to these rules, and one draw needn't show every extreme that they name: `routes`: each row names 8 different experts. Among the 512 rows of one block no expert is named more than 48 times, a bound that some block reaches.
All inputs are finite; a program needn't handle non-finite values.
Results may differ from a plain program's by a relative error of at most 0.017.
Values may be sent and summed in bfloat16 or wider, within the bound.
A program may use at most 64 MiB of HBM per device.

v0:
```python
import jax
import jax.numpy as jnp
from jax import lax
from jax.sharding import PartitionSpec as P

CAP = 48


def in_one_piece(arrays, axis, split_dim, concat_dim, along):
    ends, at = ([], 0)
    for a in arrays[:-1]:
        at += a.shape[along]
        ends.append(at)
    both = jnp.concatenate(arrays, axis=along)
    return tuple(
        jnp.split(
            lax.all_to_all(both, axis, split_axis=split_dim, concat_axis=concat_dim, tiled=True),
            ends,
            axis=along,
        )
    )


def sent_together(arrays, axis, dim, along):
    ends, at = ([], 0)
    for a in arrays[:-1]:
        at += a.shape[along]
        ends.append(at)
    both = jnp.concatenate(arrays, axis=along)
    return tuple(jnp.split(lax.all_gather(both, axis, axis=dim, tiled=True), ends, axis=along))


def split_up(array, dim, peers):
    dims = array.shape
    pieces = array.reshape(*dims[:dim], peers, dims[dim] // peers, *dims[dim + 1 :])
    return jnp.moveaxis(pieces, dim, 0)


def sum_at_owner(array, axis, dim):
    peers = lax.axis_size(axis)
    pieces = lax.all_to_all(split_up(array, dim, peers), axis, 0, 0, tiled=True)
    return jnp.sum(pieces.astype(jnp.float32), axis=0)


def copy_for_each(array, axis):
    copies = jnp.broadcast_to(array, (lax.axis_size(axis), *array.shape))
    return lax.all_to_all(copies, axis, split_axis=0, concat_axis=0, tiled=True)


def laid_out(pieces, dim):
    pieces = jnp.moveaxis(pieces, 0, dim)
    dims = pieces.shape
    return pieces.reshape(*dims[:dim], dims[dim] * dims[dim + 1], *dims[dim + 2 :])


def collect(array, axis, dim):
    pieces = copy_for_each(array, axis)
    return laid_out(pieces, dim)


def taken_together(array, axis):
    everything = copy_for_each(array, axis)
    return jnp.sum(everything, axis=0)


def silu_parts(gate_pre):
    sigmoid_val = jax.nn.sigmoid(gate_pre)
    return (gate_pre * sigmoid_val, sigmoid_val * (1.0 + gate_pre * (1.0 - sigmoid_val)))


def body(tokens, grad_out, routes, gates, gate_weight, up_weight, down_weight):
    tok_rows = tokens.shape[0]
    route_count = routes.shape[1]
    groups = lax.axis_size("tensor")
    hid_dev = gate_weight.shape[1]
    capacity = CAP
    contract = (((1,), (1,)), ((), ()))
    pick_dims = (((0,), (0,)), ((), ()))
    first_id = lax.axis_index("expert") * groups
    local_ids = first_id + jnp.arange(groups, dtype=jnp.int32)
    flat_ids = routes.reshape(-1)
    onehot = (flat_ids[:, None] == local_ids[None, :]).astype(jnp.int32)
    ranking = jnp.sum((jnp.cumsum(onehot, axis=0) - 1) * onehot, axis=1)
    position = jnp.sum(onehot * jnp.arange(groups, dtype=jnp.int32)[None, :], axis=1)
    inside = jnp.sum(onehot, axis=1) > 0
    slot_ids = jnp.where(inside, position * capacity + ranking, -1).reshape(tok_rows, -1)
    slot_iota = jnp.arange(groups * capacity, dtype=jnp.int32)
    weighted = jnp.zeros((tok_rows, groups * capacity), jnp.float32)
    slot_hits = jnp.zeros((tok_rows, groups * capacity), jnp.float32)
    for route_col in range(route_count):
        matches = slot_ids[:, route_col, None] == slot_iota[None, :]
        weighted = weighted + jnp.where(matches, gates[:, route_col, None], 0.0)
        slot_hits = slot_hits + matches.astype(jnp.float32)
    weight_map = weighted.astype(jnp.bfloat16)
    picker = slot_hits.astype(jnp.bfloat16)
    tok_slots = (
        lax.dot_general(picker, tokens, pick_dims, preferred_element_type=jnp.float32)
        .astype(jnp.bfloat16)
        .reshape(groups, capacity, -1)
    )
    grad_slots = (
        lax.dot_general(picker, grad_out, pick_dims, preferred_element_type=jnp.float32)
        .astype(jnp.bfloat16)
        .reshape(groups, capacity, -1)
    )
    w_gate = gate_weight[0]
    w_up = up_weight[0]
    w_down = down_weight[0]
    tok_full, grad_full = in_one_piece((tok_slots, grad_slots), "tensor", 0, 2, 1)
    grad_own = grad_full[0]
    tok_all, grad_all = sent_together((tok_full[0], grad_own), "dp", 0, 1)
    gate_part = lax.dot_general(tok_all, w_gate, contract, preferred_element_type=jnp.float32)
    up_part = lax.dot_general(tok_all, w_up, contract, preferred_element_type=jnp.float32)
    projected = jnp.concatenate([gate_part, up_part], axis=1)
    gate_pre = projected[:, :hid_dev]
    up_pre = projected[:, hid_dev:]
    activated, slope_val = silu_parts(gate_pre)
    hidden = (activated * up_pre).astype(jnp.bfloat16)
    row_block = hidden
    expert_out = sum_at_owner(
        jnp.dot(row_block, w_down, preferred_element_type=jnp.float32).astype(jnp.bfloat16), "dp", 0
    ).astype(jnp.bfloat16)
    returned = lax.all_to_all(
        expert_out[None], "tensor", split_axis=2, concat_axis=0, tiled=True
    ).reshape(groups * capacity, -1)
    out_part = jnp.dot(weight_map, returned, preferred_element_type=jnp.float32)
    out_share = sum_at_owner(out_part.astype(jnp.bfloat16), "expert", 0).astype(jnp.bfloat16)
    mixed = collect(out_share, "expert", 0)
    gate_scale = up_pre * slope_val
    grad_hid = lax.dot_general(grad_all, w_down, contract, preferred_element_type=jnp.float32)
    grad_gate = (grad_hid * gate_scale).astype(jnp.bfloat16)
    grad_up = (grad_hid * activated).astype(jnp.bfloat16)
    grad_joint = jnp.concatenate([grad_gate, grad_up], axis=1)
    stacked = jnp.concatenate([w_gate, w_up], axis=0)
    row_block = grad_joint
    expert_back = lax.psum_scatter(
        jnp.dot(row_block, stacked, preferred_element_type=jnp.float32).astype(jnp.bfloat16),
        "dp",
        scatter_dimension=0,
        tiled=True,
    )
    back_slots = lax.all_to_all(
        expert_back[None], "tensor", split_axis=2, concat_axis=0, tiled=True
    ).reshape(groups * capacity, -1)
    grad_part = jnp.dot(weight_map, back_slots, preferred_element_type=jnp.float32)
    grad_share = sum_at_owner(grad_part.astype(jnp.bfloat16), "expert", 0).astype(jnp.bfloat16)
    grad_tokens = collect(grad_share, "expert", 0)
    slot_grads = jnp.sum(expert_out.astype(jnp.float32) * grad_own.astype(jnp.float32), axis=1)
    own_slots = lax.axis_index("tensor") * capacity + jnp.arange(capacity, dtype=jnp.int32)
    columns = []
    for route_col in range(route_count):
        matches = slot_ids[:, route_col, None] == own_slots[None, :]
        columns.append(jnp.sum(jnp.where(matches, slot_grads[None, :], 0.0), axis=1))
    gate_part = jnp.stack(columns, axis=1)
    grad_gates = taken_together(gate_part, ("expert", "tensor"))
    return (mixed, grad_tokens, grad_gates)


def solution(mesh):
    return jax.shard_map(
        body,
        mesh=mesh,
        in_specs=(
            P("dp", "tensor"),
            P("dp", "tensor"),
            P("dp", None),
            P("dp", None),
            P(("expert", "tensor"), "dp", None),
            P(("expert", "tensor"), "dp", None),
            P(("expert", "tensor"), "dp", None),
        ),
        out_specs=(P("dp", "tensor"), P("dp", "tensor"), P("dp", None)),
        check_vma=False,
    )
```

profile of v0, /device:TPU:8, one launch (start us, length us, event | category | flops | bytes accessed | tf_op | source)
XLA Modules:
  0.0 331.4 jit_solution(5535200742972902015)
XLA Ops:
  13.8 25.6 %all_to_all.78 = bf16[4,96,512]{2,1,0:T(8,128)(2,1)S(1)} all-to-all(bf16[4,96,512]{2,1,0:T(8,128)(2,1)S(1)} %pad_maximum_fusion), channel_id=1, replica_groups=mesh['dp'=8,'tensor'=4,'expert'=16] {'tensor'}, dimensions={0} | all-to-all | bytes 786432 | tf_op jit(solution)/shard_map/all_to_all | solution.py:17
  40.3 44.9 %all-gather.2.cloned.1.call-done = bf16[384,4096]{1,0:T(8,128)(2,1)} async-done(((bf16[48,4096]{1,0:T(8,128)(2,1)}), bf16[384,4096]{1,0:T(8,128)(2,1)}) %all-gather.2.cloned.1.call-update) | async-done | bytes 3145744 | tf_op jit(solution)/shard_map/all_gather | solution.py:30
  85.3 2.1 fusion.5
  87.4 2.2 fusion.7
  90.4 2.2 convolution_convert_fusion
  93.3 56.7 %all_to_all.79 = bf16[8,48,2048]{2,1,0:T(8,128)(2,1)S(1)} all-to-all(bf16[8,48,2048]{2,1,0:T(8,128)(2,1)S(1)} %bitcast.72), channel_id=1, replica_groups=mesh['dp'=8,'tensor'=4,'expert'=16] {'dp'}, dimensions={0} | all-to-all | bytes 3145728 | tf_op jit(solution)/shard_map/all_to_all | solution.py:41
  151.5 11.5 %reduce.21 = bf16[2048,48]{1,0:T(8,128)(2,1)S(1)} reduce(bf16[2048,1,48]{2,1,0:T(2,128)(2,1)S(1)} %bitcast.75, bf16[]{:T(256)} %broadcast.68), dimensions={1}, to_apply=%bitcast.61.reduce_sub_computation | reduce | bytes 393218
  164.5 7.4 %all-to-all-start.2 = ((bf16[4,2,12288]{2,1,0:T(2,128)(2,1)}), bf16[4,2,12288]{2,1,0:T(2,128)(2,1)S(1)}, u32[]{:S(2)}, u32[]{:S(2)}) async-start(bf16[4,2,12288]{2,1,0:T(2,128)(2,1)} %reshape.95), calls=%async_computation.2 | async-start | bytes 393216 | tf_op jit(solution)/shard_map/all_to_all | solution.py:123
  171.9 2.1 copy.37
  174.0 11.5 %reduce.22 = bf16[2048,48]{1,0:T(8,128)(2,1)S(1)} reduce(bf16[2048,1,48]{2,1,0:T(2,128)(2,1)S(1)} %bitcast.76, bf16[]{:T(256)} %broadcast.68), dimensions={1}, to_apply=%bitcast.63.reduce_sub_computation | reduce | bytes 393218
  187.1 7.2 %all-to-all-start.5 = ((bf16[4,2,12288]{2,1,0:T(2,128)(2,1)}), bf16[4,2,12288]{2,1,0:T(2,128)(2,1)S(1)}, u32[]{:S(2)}, u32[]{:S(2)}) async-start(bf16[4,2,12288]{2,1,0:T(2,128)(2,1)} %reshape.97), calls=%async_computation.6 | async-start | bytes 393216 | tf_op jit(solution)/shard_map/all_to_all | solution.py:142
  196.1 2.7 convolution_convert_fusion.3
  198.8 4.7 %all-to-all-done.5 = bf16[4,2,12288]{2,1,0:T(2,128)(2,1)S(1)} async-done(((bf16[4,2,12288]{2,1,0:T(2,128)(2,1)}), bf16[4,2,12288]{2,1,0:T(2,128)(2,1)S(1)}, u32[]{:S(2)}, u32[]{:S(2)}) %all-to-all-start.5) | async-done | bytes 196640 | tf_op jit(solution)/shard_map/all_to_all | solution.py:142
  203.6 6.7 %all-to-all-start.3 = ((bf16[16,32,512]{2,1,0:T(8,128)(2,1)}), bf16[16,32,512]{2,1,0:T(8,128)(2,1)S(1)}, u32[]{:S(2)}, u32[]{:S(2)}) async-start(bf16[16,32,512]{2,1,0:T(8,128)(2,1)} %bitcast.22), calls=%async_computation.3 | async-start | bytes 1048576 | tf_op jit(solution)/shard_map/all_to_all | solution.py:41
  212.1 2.7 convolution_convert_fusion.2
  214.9 11.6 %all-to-all-done.3 = bf16[16,32,512]{2,1,0:T(8,128)(2,1)S(1)} async-done(((bf16[16,32,512]{2,1,0:T(8,128)(2,1)}), bf16[16,32,512]{2,1,0:T(8,128)(2,1)S(1)}, u32[]{:S(2)}, u32[]{:S(2)}) %all-to-all-start.3) | async-done | bytes 524320 | tf_op jit(solution)/shard_map/all_to_all | solution.py:41
  226.5 3.6 %all-to-all-start.6 = ((bf16[16,32,512]{2,1,0:T(8,128)(2,1)}), bf16[16,32,512]{2,1,0:T(8,128)(2,1)S(1)}, u32[]{:S(2)}, u32[]{:S(2)}) async-start(bf16[16,32,512]{2,1,0:T(8,128)(2,1)} %bitcast.27), calls=%async_computation.7 | async-start | bytes 1048576 | tf_op jit(solution)/shard_map/all_to_all | solution.py:41
  230.5 15.3 %all-to-all-done.6 = bf16[16,32,512]{2,1,0:T(8,128)(2,1)S(1)} async-done(((bf16[16,32,512]{2,1,0:T(8,128)(2,1)}), bf16[16,32,512]{2,1,0:T(8,128)(2,1)S(1)}, u32[]{:S(2)}, u32[]{:S(2)}) %all-to-all-start.6) | async-done | bytes 524320 | tf_op jit(solution)/shard_map/all_to_all | solution.py:41
  246.9 4.7 %all-to-all-start.8 = ((f32[64,512,8]{1,2,0:T(8,128)}), f32[64,512,8]{1,2,0:T(8,128)S(1)}, u32[]{:S(2)}, u32[]{:S(2)}) async-start(f32[64,512,8]{1,2,0:T(8,128)} %broadcast_in_dim.179), calls=%async_computation.9 | async-start | bytes 2097152 | tf_op jit(solution)/shard_map/all_to_all | solution.py:47
  251.7 28.7 %all-to-all-done.8 = f32[64,512,8]{1,2,0:T(8,128)S(1)} async-done(((f32[64,512,8]{1,2,0:T(8,128)}), f32[64,512,8]{1,2,0:T(8,128)S(1)}, u32[]{:S(2)}, u32[]{:S(2)}) %all-to-all-start.8) | async-done | bytes 1048608 | tf_op jit(solution)/shard_map/all_to_all | solution.py:47
  281.2 4.7 %all-to-all-start.4 = ((bf16[16,32,512]{2,1,0:T(8,128)(2,1)}), bf16[16,32,512]{2,1,0:T(8,128)(2,1)S(1)}, u32[]{:S(2)}, u32[]{:S(2)}) async-start(bf16[16,32,512]{2,1,0:T(8,128)(2,1)} %broadcast_in_dim.174), calls=%async_computation.4 | async-start | bytes 1048576 | tf_op jit(solution)/shard_map/all_to_all | solution.py:47
  286.1 16.5 %all-to-all-done.4 = bf16[16,32,512]{2,1,0:T(8,128)(2,1)S(1)} async-done(((bf16[16,32,512]{2,1,0:T(8,128)(2,1)}), bf16[16,32,512]{2,1,0:T(8,128)(2,1)S(1)}, u32[]{:S(2)}, u32[]{:S(2)}) %all-to-all-start.4) | async-done | bytes 524320 | tf_op jit(solution)/shard_map/all_to_all | solution.py:47
  303.4 3.6 %all-to-all-start.7 = ((bf16[16,32,512]{2,1,0:T(8,128)(2,1)}), bf16[16,32,512]{2,1,0:T(8,128)(2,1)S(1)}, u32[]{:S(2)}, u32[]{:S(2)}) async-start(bf16[16,32,512]{2,1,0:T(8,128)(2,1)} %broadcast_in_dim.176), calls=%async_computation.8 | async-start | bytes 1048576 | tf_op jit(solution)/shard_map/all_to_all | solution.py:47
  307.7 15.3 %all-to-all-done.7 = bf16[16,32,512]{2,1,0:T(8,128)(2,1)S(1)} async-done(((bf16[16,32,512]{2,1,0:T(8,128)(2,1)}), bf16[16,32,512]{2,1,0:T(8,128)(2,1)S(1)}, u32[]{:S(2)}, u32[]{:S(2)}) %all-to-all-start.7) | async-done | bytes 524320 | tf_op jit(solution)/shard_map/all_to_all | solution.py:47
  (67 shorter events, 22.6 us)
Async XLA Ops:
  7.2 82.4 %copy-start = (bf16[1,192,2048]{2,1,0:T(8,128)(2,1)S(1)}, bf16[1,192,2048]{2,1,0:T(8,128)(2,1)}, u32[]{:S(2)}) copy-start(bf16[1,192,2048]{2,1,0:T(8,128)(2,1)} %param.13) | copy-start | bytes 2359300
  7.2 78.1 %all-gather.2.cloned.1.call-start = ((), (), s32[]{:S(2)}) async-start(), calls=%async_computation.10 | async-start | bytes 3538944 | tf_op jit(solution)/shard_map/all_gather | solution.py:30
  8.4 3.3 copy-start.5
  11.7 1.0 copy-start.6
  39.4 45.9 %copy-start.1 = (bf16[1,192,2048]{2,1,0:T(8,128)(2,1)S(1)}, bf16[1,192,2048]{2,1,0:T(8,128)(2,1)}, u32[]{:S(2)}) copy-start(bf16[1,192,2048]{2,1,0:T(8,128)(2,1)} %param.12) | copy-start | bytes 2359300
  40.3 47.1 %copy-start.2 = (bf16[1,192,2048]{2,1,0:T(8,128)(2,1)S(1)}, bf16[1,192,2048]{2,1,0:T(8,128)(2,1)}, u32[]{:S(2)}) copy-start(bf16[1,192,2048]{2,1,0:T(8,128)(2,1)} %param.11) | copy-start | bytes 2359300
  40.3 131.6 %reduce-scatter.2.cloned.1.call-start = ((), (), s32[]{:S(2)}) async-start(), calls=%async_computation.11 | async-start | bytes 1769472 | tf_op jit(solution)/shard_map/reduce_scatter | solution.py:136
  87.4 2.4 copy-start.4
  164.5 22.6 %all-to-all-start.2 = ((bf16[4,2,12288]{2,1,0:T(2,128)(2,1)}), bf16[4,2,12288]{2,1,0:T(2,128)(2,1)S(1)}, u32[]{:S(2)}, u32[]{:S(2)}) async-start(bf16[4,2,12288]{2,1,0:T(2,128)(2,1)} %reshape.95), calls=%async_computation.2 | async-start | bytes 393216 | tf_op jit(solution)/shard_map/all_to_all | solution.py:123
  174.0 20.3 %copy-start.3 = (f32[512,8]{0,1:T(8,128)S(1)}, f32[512,8]{0,1:T(8,128)}, u32[]{:S(2)}) copy-start(f32[512,8]{0,1:T(8,128)} %param.10) | copy-start | bytes 49156
  187.1 16.5 %all-to-all-start.5 = ((bf16[4,2,12288]{2,1,0:T(2,128)(2,1)}), bf16[4,2,12288]{2,1,0:T(2,128)(2,1)S(1)}, u32[]{:S(2)}, u32[]{:S(2)}) async-start(bf16[4,2,12288]{2,1,0:T(2,128)(2,1)} %reshape.97), calls=%async_computation.6 | async-start | bytes 393216 | tf_op jit(solution)/shard_map/all_to_all | solution.py:142
  203.6 22.9 %all-to-all-start.3 = ((bf16[16,32,512]{2,1,0:T(8,128)(2,1)}), bf16[16,32,512]{2,1,0:T(8,128)(2,1)S(1)}, u32[]{:S(2)}, u32[]{:S(2)}) async-start(bf16[16,32,512]{2,1,0:T(8,128)(2,1)} %bitcast.22), calls=%async_computation.3 | async-start | bytes 1048576 | tf_op jit(solution)/shard_map/all_to_all | solution.py:41
  226.5 19.3 %all-to-all-start.6 = ((bf16[16,32,512]{2,1,0:T(8,128)(2,1)}), bf16[16,32,512]{2,1,0:T(8,128)(2,1)S(1)}, u32[]{:S(2)}, u32[]{:S(2)}) async-start(bf16[16,32,512]{2,1,0:T(8,128)(2,1)} %bitcast.27), calls=%async_computation.7 | async-start | bytes 1048576 | tf_op jit(solution)/shard_map/all_to_all | solution.py:41
  246.9 33.5 %all-to-all-start.8 = ((f32[64,512,8]{1,2,0:T(8,128)}), f32[64,512,8]{1,2,0:T(8,128)S(1)}, u32[]{:S(2)}, u32[]{:S(2)}) async-start(f32[64,512,8]{1,2,0:T(8,128)} %broadcast_in_dim.179), calls=%async_computation.9 | async-start | bytes 2097152 | tf_op jit(solution)/shard_map/all_to_all | solution.py:47
  281.2 21.3 %all-to-all-start.4 = ((bf16[16,32,512]{2,1,0:T(8,128)(2,1)}), bf16[16,32,512]{2,1,0:T(8,128)(2,1)S(1)}, u32[]{:S(2)}, u32[]{:S(2)}) async-start(bf16[16,32,512]{2,1,0:T(8,128)(2,1)} %broadcast_in_dim.174), calls=%async_computation.4 | async-start | bytes 1048576 | tf_op jit(solution)/shard_map/all_to_all | solution.py:47
  303.4 19.6 %all-to-all-start.7 = ((bf16[16,32,512]{2,1,0:T(8,128)(2,1)}), bf16[16,32,512]{2,1,0:T(8,128)(2,1)S(1)}, u32[]{:S(2)}, u32[]{:S(2)}) async-start(bf16[16,32,512]{2,1,0:T(8,128)(2,1)} %broadcast_in_dim.176), calls=%async_computation.8 | async-start | bytes 1048576 | tf_op jit(solution)/shard_map/all_to_all | solution.py:47
Sparse Core Ops, SparseCore 0:
  40.4 44.8 all-gather.1
  92.8 58.7 reduce-scatter.1
where the time goes:
time: 333 us; the launch traced here: 331 us
  waiting for transfers between devices  137 us (41%)
  blocking collectives  82.3 us (25%)
  starting transfers between devices  37.9 us (11%)
  other arithmetic  27.1 us (8%)
  local copies, waits for them, and re-layouts  17.3 us (5%)
  matrix products  15.2 us (5%)
  between operations  14.4 us (4%)
    all_to_all x3, waiting for transfers between devices, copy_for_each(): return lax.all_to_all(copies, axis, split_axis=0, concat_axis=0, tiled=True)  60.6 us
    all_to_all x1, blocking collectives, sum_at_owner(): pieces = lax.all_to_all(split_up(array, dim, peers), axis, 0, 0, tiled=True)  56.7 us
    all_gather x1, waiting for transfers between devices, sent_together(): lax.all_gather(both, axis, axis=dim, tiled=True)  44.9 us
    all_to_all x2, waiting for transfers between devices, sum_at_owner(): pieces = lax.all_to_all(split_up(array, dim, peers), axis, 0, 0, tiled=True)  26.9 us
    all_to_all x1, blocking collectives, in_one_piece(): lax.all_to_all(both, axis, split_axis=split_dim, concat_axis=concat_dim,...  25.6 us
    unnamed x3, other arithmetic  23.2 us
    all_to_all x3, starting transfers between devices, copy_for_each(): return lax.all_to_all(copies, axis, split_axis=0, concat_axis=0, tiled=True)  13 us
    all_to_all x2, starting transfers between devices, sum_at_owner(): pieces = lax.all_to_all(split_up(array, dim, peers), axis, 0, 0, tiled=True)  10.3 us
  transfers between devices with their start and end apart: 9, of which 7 were waited for; matrix products, arithmetic and copies ran while one was open for 12% of the time, Pallas kernels for 0%

commit v1 on v0

v1 whole, which is shorter than its diff:
```python
import jax
import jax.numpy as jnp
from jax import lax
from jax.experimental import pallas as pl
from jax.experimental.pallas import tpu as pltpu
from jax.sharding import PartitionSpec as P

CAP = 48
MESH = pl.DeviceIdType.MESH
F32 = jnp.float32
BF16 = jnp.bfloat16
NT = (((1,), (1,)), ((), ()))
TN = (((0,), (0,)), ((), ()))
ANTI = 7


def dot(a, b):
    return jnp.dot(a, b, preferred_element_type=F32)


def dot_nt(a, b):
    return lax.dot_general(a, b, NT, preferred_element_type=F32)


def dot_tn(a, b):
    return lax.dot_general(a, b, TN, preferred_element_type=F32)


def kernel(
    routes, gates, tok, grad, wg_hbm, wu_hbm, wd_hbm,
    mixed, grad_tokens, grad_gates_t,
    wg, wu, wd, ag, picked, act, scl, hid, gg, gu, pb, rs_rx, rs_tx,
    ret, ret_tx, pick_t, wm_t, ids_t, xs_tx, xs_rx, zacc, zs_tx, zs_rx, res,
    g_tx, g_rx, g_all,
    w_sem, ag_s, ag_r, rs_s, rs_r, pk_s, pk_r, rt_s, rt_r,
    xs_s, xs_r, zs_s, zs_r, za_s, za_r, xa_s, xa_r, g1_s, g1_r, g2_s, g2_r, g3_s, g3_r,
):
    y, t, e = lax.axis_index("dp"), lax.axis_index("tensor"), lax.axis_index("expert")
    n_dp = 8
    zh, core = t // 2, t % 2
    x, zl = e // 4, e % 4
    mirror = x * 4 + 3 - zl
    t1 = 2 * zh + 1 - core
    t2 = 2 * (1 - zh) + core
    t3 = 2 * (1 - zh) + 1 - core
    feats = (t, t1, t2, t3)
    experts = (4 * e + t, 4 * e + t1, 4 * mirror + t2, 4 * mirror + t3)
    peers = (None, (y, t1, e), (y, t2, mirror), (y, t3, mirror))
    up = (lax.rem(y + 1, n_dp), t, e)
    down = (lax.rem(y + n_dp - 1, n_dp), t, e)
    ring = (up, down)
    x_at = [lax.rem(x + rel, 4) for rel in range(4)]
    z_at = [lax.rem(zl + rel, 4) for rel in range(4)]
    x_peers = [(y, t, x_at[rel] * 4 + zl) for rel in range(4)]
    z_peers = [(y, t, x * 4 + z_at[rel]) for rel in range(4)]

    started = []

    def send(src, dst, s, r, to):
        copy = pltpu.make_async_remote_copy(
            src_ref=src, dst_ref=dst, send_sem=s, recv_sem=r, device_id=to, device_id_type=MESH
        )
        copy.start()
        started.append(copy)
        return copy

    loads = []
    for n, (hbm, vmem) in enumerate(((wg_hbm, wg), (wu_hbm, wu), (wd_hbm, wd))):
        for j in range(4):
            at = pl.multiple_of(feats[j] * 512, 512)
            load = pltpu.make_async_copy(hbm.at[0, :, pl.ds(at, 512)], vmem.at[j], w_sem.at[n, j])
            load.start()
            loads.append(load)

    barrier = pltpu.get_barrier_semaphore()
    everyone = list(ring) + list(peers[1:]) + x_peers[1:] + z_peers[1:]
    for peer in everyone:
        pl.semaphore_signal(barrier, inc=1, device_id=peer, device_id_type=MESH)

    eye = (
        lax.broadcasted_iota(jnp.int32, (8, 8), 0) == lax.broadcasted_iota(jnp.int32, (8, 8), 1)
    ).astype(F32).astype(BF16)
    ids = dot_nt(eye, routes[...].astype(F32).astype(BF16)).astype(jnp.int32)
    gate_rows = dot_nt(eye, gates[...].astype(BF16))
    ids_t[...] = ids
    row8 = lax.broadcasted_iota(jnp.int32, (8, 512), 0)
    masks = []
    chosen = jnp.zeros((8, 512), F32)
    for q in range(4):
        mask = jnp.sum((ids == experts[q]).astype(F32), axis=0, keepdims=True)
        masks.append(mask)
        chosen = chosen + jnp.where(row8 == q, mask, 0.0)
    before = (
        lax.broadcasted_iota(jnp.int32, (512, 512), 0) < lax.broadcasted_iota(jnp.int32, (512, 512), 1)
    ).astype(F32).astype(BF16)
    rank = dot(chosen.astype(BF16), before).astype(jnp.int32)
    slot = lax.broadcasted_iota(jnp.int32, (CAP, 512), 0)
    for q in range(4):
        hit = (slot == rank[q : q + 1]) & (masks[q] > 0.0)
        gate = jnp.sum(jnp.where(ids == experts[q], gate_rows, 0.0), axis=0, keepdims=True)
        pick_t[48 * q : 48 * q + 48] = jnp.where(hit, 1.0, 0.0).astype(BF16)
        wm_t[48 * q : 48 * q + 48] = jnp.where(hit, gate, 0.0).astype(BF16)

    ag_copy, pk_copy = {}, {}

    def ag_send(kind, way, d, j, src, dst):
        ag_copy[kind, way, d, j] = send(
            ag.at[kind, j, src], ag.at[kind, j, dst],
            ag_s.at[kind, way, d, j], ag_r.at[kind, way, d, j], ring[way],
        )

    def send_own(kind, j):
        ag_send(kind, 0, 0, j, 0, 1)
        ag_send(kind, 1, 0, j, 0, 2)

    for kind, rows in ((0, tok), (1, grad)):
        got = dot(pick_t[...], rows[...]).astype(BF16)
        ag[kind, 0, 0] = got[0:48]
        for q in (2, 3, 1):
            picked[kind, q - 1] = got[48 * q : 48 * q + 48]
        if kind == 0:
            pl.semaphore_wait(barrier, len(everyone))
        for q in (2, 3, 1):
            pk_copy[kind, q] = send(
                picked.at[kind, q - 1], ag.at[kind, q, 0], pk_s.at[kind, q - 1], pk_r.at[kind, q - 1], peers[q]
            )
        send_own(kind, 0)

    def own_in(kind, j):
        pk_copy[kind, j].wait_recv()
        send_own(kind, j)

    own_in(0, 1)
    own_in(1, 1)
    own_in(0, 2)
    own_in(0, 3)
    for load in loads:
        load.wait()

    def rows_of(kind, j, s0, n):
        return ag[kind, j, s0 : s0 + n].reshape(n * CAP, 512)

    tasks = []

    def forward(s0, n):
        def first():
            gate_pre = dot_nt(rows_of(0, 0, s0, n), wg[0])
            for j in range(1, 4):
                gate_pre = gate_pre + dot_nt(rows_of(0, j, s0, n), wg[j])
            sig = jax.nn.sigmoid(gate_pre)
            act[s0 : s0 + n] = (gate_pre * sig).reshape(n, CAP, 192)
            scl[s0 : s0 + n] = (sig * (1.0 + gate_pre * (1.0 - sig))).reshape(n, CAP, 192)

        def second():
            up_pre = dot_nt(rows_of(0, 0, s0, n), wu[0])
            for j in range(1, 4):
                up_pre = up_pre + dot_nt(rows_of(0, j, s0, n), wu[j])
            up_pre = up_pre.reshape(n, CAP, 192)
            hid[s0 : s0 + n] = (act[s0 : s0 + n] * up_pre).astype(BF16)
            scl[s0 : s0 + n] = up_pre * scl[s0 : s0 + n]

        def third(j):
            out = dot(hid[s0 : s0 + n].reshape(n * CAP, 192), wd[j])
            pb[0, s0 : s0 + n, j] = out.astype(BF16).reshape(n, CAP, 512)

        return [first, second] + [lambda j=j: third(j) for j in range(4)]

    def backward(s0, n):
        def first():
            grad_hid = dot_nt(rows_of(1, 0, s0, n), wd[0])
            for j in range(1, 4):
                grad_hid = grad_hid + dot_nt(rows_of(1, j, s0, n), wd[j])
            grad_hid = grad_hid.reshape(n, CAP, 192)
            gg[s0 : s0 + n] = (grad_hid * scl[s0 : s0 + n]).astype(BF16)
            gu[s0 : s0 + n] = (grad_hid * act[s0 : s0 + n]).astype(BF16)

        def second(j):
            back = dot(gg[s0 : s0 + n].reshape(n * CAP, 192), wg[j])
            back = back + dot(gu[s0 : s0 + n].reshape(n * CAP, 192), wu[j])
            pb[1, s0 : s0 + n, j] = back.astype(BF16).reshape(n, CAP, 512)

        return [first] + [lambda j=j: second(j) for j in range(4)]

    def work(n):
        for _ in range(min(n, len(tasks))):
            tasks.pop(0)()

    def gather(kind, make):
        for d in range(1, 5):
            for j in range(4):
                for way in range(2):
                    if d == 4 and (j < 2) != (way == 0):
                        continue
                    ag_copy[kind, way, d - 1, j].wait_recv()
                    if d < 3:
                        ag_send(kind, way, d, j, 2 * d - 1 + way, 2 * d + 1 + way)
                    elif d == 3 and (j < 2) == (way == 0):
                        ag_send(kind, way, d, j, 2 * d - 1 + way, ANTI)
                if kind == 1 and d == 3 and j == 3:
                    scatter_first(0)
                work(2)
            tasks.extend(make(2 * d - 1, 2) if d < 4 else make(ANTI, 1))

    rs_copy = {}

    def rs_send(kind, way, s, j, src):
        rs_copy[kind, way, s, j] = send(
            src, rs_rx.at[kind, way, s, j], rs_s.at[kind, way, s, j], rs_r.at[kind, way, s, j], ring[way]
        )

    def scatter_first(kind):
        for j in range(2):
            rs_send(kind, 0, 0, j, pb.at[kind, ANTI, j])
            rs_send(kind, 1, 0, j + 2, pb.at[kind, ANTI, j + 2])

    def scatter(kind, s, busy):
        d = 4 - s
        for j in range(4):
            for way in range(2):
                at = 2 * d if way == 0 else 2 * d - 1
                if s == 1 and (j < 2) != (way == 0):
                    rs_send(kind, way, s, j, pb.at[kind, at, j])
                    continue
                rs_copy[kind, way, s - 1, j].wait_recv()
                rs_tx[kind, way, s - 1, j] = (
                    pb[kind, at, j].astype(F32) + rs_rx[kind, way, s - 1, j].astype(F32)
                ).astype(BF16)
                rs_send(kind, way, s, j, rs_tx.at[kind, way, s - 1, j])
            work(busy)

    rt_copy = {}

    def home(kind):
        products = None
        for j in (2, 3, 1, 0):
            for way in range(2):
                rs_copy[kind, way, 3, j].wait_recv()
            total = (
                pb[kind, 0, j].astype(F32)
                + rs_rx[kind, 0, 3, j].astype(F32)
                + rs_rx[kind, 1, 3, j].astype(F32)
            ).astype(BF16)
            if j == 0:
                ret[kind, 0:48] = total
            else:
                ret_tx[kind, j - 1] = total
                rt_copy[kind, j] = send(
                    ret_tx.at[kind, j - 1], ret.at[kind, pl.ds(48 * j, 48)],
                    rt_s.at[kind, j - 1], rt_r.at[kind, j - 1], peers[j],
                )
            if kind == 0:
                term = jnp.sum(total.astype(F32) * ag[1, j, 0].astype(F32), axis=1, keepdims=True)
                products = term if products is None else products + term
        if kind == 0:
            own = jnp.sum(pick_t[0:48].astype(F32) * products, axis=0, keepdims=True)
            g_tx[0] = jnp.broadcast_to(own, (8, 512))
            for j in (2, 3, 1):
                g_copy[1, j] = send(g_tx.at[0], g_rx.at[j - 1], g1_s.at[j - 1], g1_r.at[j - 1], peers[j])

    g_copy, e_copy = {}, {}

    def gates_second():
        block = jnp.where(row8 == 0, g_tx[0], 0.0)
        for j in range(1, 4):
            g_copy[1, j].wait_recv()
            block = block + jnp.where(row8 == j, g_rx[j - 1], 0.0)
        g_tx[1] = block
        g_all[zl, x] = block
        for rel in range(1, 4):
            g_copy[2, rel] = send(
                g_tx.at[1], g_all.at[zl, x], g2_s.at[rel - 1], g2_r.at[rel - 1], x_peers[rel]
            )

    def gates_third():
        for rel in range(1, 4):
            g_copy[2, rel].wait_recv()
        for rel in range(1, 4):
            g_copy[3, rel] = send(
                g_all.at[zl], g_all.at[zl], g3_s.at[rel - 1], g3_r.at[rel - 1], z_peers[rel]
            )

    def gates_last():
        for rel in range(1, 4):
            g_copy[3, rel].wait_recv()
        ids_now = ids_t[...]
        sums = [jnp.zeros((8, 512), F32) for _ in range(8)]
        for zz in range(4):
            for xx in range(4):
                there, opposite = 4 * (xx * 4 + zz), 4 * (xx * 4 + 3 - zz)
                names = jnp.where(row8 == 0, there + t, -1)
                names = jnp.where(row8 == 1, there + t1, names)
                names = jnp.where(row8 == 2, opposite + t2, names)
                names = jnp.where(row8 == 3, opposite + t3, names)
                block = g_all[zz, xx]
                for r in range(8):
                    sums[r] = sums[r] + jnp.where(ids_now[r : r + 1] == names, block, 0.0)
        for r in range(8):
            grad_gates_t[r : r + 1] = jnp.sum(sums[r], axis=0, keepdims=True)

    def cols(at):
        return pl.ds(pl.multiple_of(at * 128, 128), 128)

    def x_scatter(kind):
        for j in range(1, 4):
            rt_copy[kind, j].wait_recv()
        for rel in (2, 1, 3):
            part = dot_tn(wm_t[:, cols(x_at[rel])], ret[kind])
            xs_tx[kind, rel - 1] = part.astype(BF16)
            e_copy["xs", kind, rel] = send(
                xs_tx.at[kind, rel - 1], xs_rx.at[kind, rel - 1],
                xs_s.at[kind, rel - 1], xs_r.at[kind, rel - 1], x_peers[rel],
            )
        zacc[kind] = dot_tn(wm_t[:, cols(x)], ret[kind])

    def z_scatter(kind):
        for rel in (1, 3, 2):
            e_copy["xs", kind, rel].wait_recv()
        total = zacc[kind]
        for rel in range(1, 4):
            total = total + xs_rx[kind, rel - 1].astype(F32)
        zacc[kind] = total
        zs_tx[kind] = total.astype(BF16)
        for rel in (2, 1, 3):
            rows = pl.ds(pl.multiple_of(z_at[rel] * 32, 32), 32)
            e_copy["zs", kind, rel] = send(
                zs_tx.at[kind, rows], zs_rx.at[kind, rel - 1],
                zs_s.at[kind, rel - 1], zs_r.at[kind, rel - 1], z_peers[rel],
            )

    def z_gather(kind):
        total = zacc[kind, pl.ds(pl.multiple_of(zl * 32, 32), 32)]
        for rel in (1, 3, 2):
            e_copy["zs", kind, rel].wait_recv()
        for rel in range(1, 4):
            total = total + zs_rx[kind, rel - 1].astype(F32)
        rows = pl.ds(pl.multiple_of(x * 128 + zl * 32, 32), 32)
        res[kind, rows] = total.astype(BF16)
        for rel in (2, 1, 3):
            e_copy["za", kind, rel] = send(
                res.at[kind, rows], res.at[kind, rows],
                za_s.at[kind, rel - 1], za_r.at[kind, rel - 1], z_peers[rel],
            )

    def x_gather(kind):
        for rel in (1, 3, 2):
            e_copy["za", kind, rel].wait_recv()
        rows = pl.ds(pl.multiple_of(x * 128, 128), 128)
        for rel in (2, 1, 3):
            e_copy["xa", kind, rel] = send(
                res.at[kind, rows], res.at[kind, rows],
                xa_s.at[kind, rel - 1], xa_r.at[kind, rel - 1], x_peers[rel],
            )

    def finish(kind, out):
        for rel in (1, 3, 2):
            e_copy["xa", kind, rel].wait_recv()
        out[...] = res[kind]

    tasks.extend(forward(0, 1))
    gather(0, forward)
    own_in(1, 2)
    own_in(1, 3)
    tasks.extend(backward(0, 1))
    gather(1, backward)
    for s in range(1, 4):
        scatter(0, s, 2)
    work(len(tasks))
    scatter_first(1)
    home(0)
    scatter(1, 1, 0)
    x_scatter(0)
    gates_second()
    scatter(1, 2, 0)
    z_scatter(0)
    gates_third()
    scatter(1, 3, 0)
    z_gather(0)
    home(1)
    x_gather(0)
    x_scatter(1)
    gates_last()
    z_scatter(1)
    finish(0, mixed)
    z_gather(1)
    x_gather(1)
    finish(1, grad_tokens)
    for copy in started:
        copy.wait_send()


def body(tokens, grad_out, routes, gates, gate_weight, up_weight, down_weight):
    vmem = pl.BlockSpec(memory_space=pltpu.VMEM)
    anywhere = pl.BlockSpec(memory_space=pl.ANY)
    dma = pltpu.SemaphoreType.DMA
    mixed, grad_tokens, grad_gates_t = pl.pallas_call(
        kernel,
        out_shape=(
            jax.ShapeDtypeStruct((512, 512), BF16),
            jax.ShapeDtypeStruct((512, 512), BF16),
            jax.ShapeDtypeStruct((8, 512), F32),
        ),
        in_specs=[vmem] * 4 + [anywhere] * 3,
        out_specs=(vmem, vmem, vmem),
        scratch_shapes=[
            pltpu.VMEM((4, 192, 512), BF16),
            pltpu.VMEM((4, 192, 512), BF16),
            pltpu.VMEM((4, 192, 512), BF16),
            pltpu.VMEM((2, 4, 8, CAP, 512), BF16),
            pltpu.VMEM((2, 3, CAP, 512), BF16),
            pltpu.VMEM((8, CAP, 192), F32),
            pltpu.VMEM((8, CAP, 192), F32),
            pltpu.VMEM((8, CAP, 192), BF16),
            pltpu.VMEM((8, CAP, 192), BF16),
            pltpu.VMEM((8, CAP, 192), BF16),
            pltpu.VMEM((2, 8, 4, CAP, 512), BF16),
            pltpu.VMEM((2, 2, 4, 4, CAP, 512), BF16),
            pltpu.VMEM((2, 2, 3, 4, CAP, 512), BF16),
            pltpu.VMEM((2, 192, 512), BF16),
            pltpu.VMEM((2, 3, CAP, 512), BF16),
            pltpu.VMEM((192, 512), BF16),
            pltpu.VMEM((192, 512), BF16),
            pltpu.VMEM((8, 512), jnp.int32),
            pltpu.VMEM((2, 3, 128, 512), BF16),
            pltpu.VMEM((2, 3, 128, 512), BF16),
            pltpu.VMEM((2, 128, 512), F32),
            pltpu.VMEM((2, 128, 512), BF16),
            pltpu.VMEM((2, 3, 32, 512), BF16),
            pltpu.VMEM((2, 512, 512), BF16),
            pltpu.VMEM((2, 8, 512), F32),
            pltpu.VMEM((3, 8, 512), F32),
            pltpu.VMEM((4, 4, 8, 512), F32),
            dma((3, 4)),
            dma((2, 2, 4, 4)),
            dma((2, 2, 4, 4)),
            dma((2, 2, 4, 4)),
            dma((2, 2, 4, 4)),
            dma((2, 3)),
            dma((2, 3)),
            dma((2, 3)),
            dma((2, 3)),
            dma((2, 3)),
            dma((2, 3)),
            dma((2, 3)),
            dma((2, 3)),
            dma((2, 3)),
            dma((2, 3)),
            dma((2, 3)),
            dma((2, 3)),
            dma((3,)),
            dma((3,)),
            dma((3,)),
            dma((3,)),
            dma((3,)),
            dma((3,)),
        ],
        compiler_params=pltpu.CompilerParams(
            collective_id=0, has_side_effects=True, vmem_limit_bytes=48 * 1024 * 1024
        ),
    )(routes, gates, tokens, grad_out, gate_weight, up_weight, down_weight)
    return mixed, grad_tokens, grad_gates_t.T


def solution(mesh):
    return jax.shard_map(
        body,
        mesh=mesh,
        in_specs=(
            P("dp", "tensor"),
            P("dp", "tensor"),
            P("dp", None),
            P("dp", None),
            P(("expert", "tensor"), "dp", None),
            P(("expert", "tensor"), "dp", None),
            P(("expert", "tensor"), "dp", None),
        ),
        out_specs=(P("dp", "tensor"), P("dp", "tensor"), P("dp", None)),
        check_vma=False,
    )
```

time: 333 us -> 135 us (0.41)
  the two profiles are of different devices: /device:TPU:8 before, /device:TPU:16 now
where the time goes in v1:
time: 135 us
  Pallas kernels  127 us (94%)
  local copies, waits for them, and re-layouts  7.66 us (6%)
    pallas_call x1, Pallas kernels, body(): pl.pallas_call(kernel, out_shape=(jax.ShapeDtypeStruct((512, 512), BF16),...  127 us
    unnamed x17, local copies, waits for them, and re-layouts  7.66 us

profile of v1, /device:TPU:16, one launch (start us, length us, event | category | flops | bytes accessed | tf_op | source)
XLA Modules:
  0.0 134.9 jit_solution(15224162392374688976)
XLA Ops:
  0.6 0.0 copy-start.5
  0.6 0.0 copy-start.3
  0.7 0.9 copy.10.routes
  1.6 0.0 copy-done.5
  1.6 0.1 copy.11.gates
  1.7 0.0 copy-done.3
  1.7 0.0 copy-start
  1.7 1.1 copy-done
  2.8 0.0 copy-start.1
  2.8 1.1 copy-done.1
  4.0 0.0 copy-start.2
  4.0 1.1 copy-done.2
  5.1 0.0 copy-start.4
  5.1 1.0 copy-done.4
  6.2 126.5 %shard_map.94 = (bf16[512,512]{1,0:T(8,128)(2,1)S(1)}, bf16[512,512]{1,0:T(8,128)(2,1)S(1)}, f32[8,512]{1,0:T(8,128)S(1)}) custom-call(s32[512,8]{1,0:T(8,128)S(1)} %copy.10.routes, f32[512,8]{1,0:T(8,128)S(1)} %copy.11.gates, bf16[512,512]{1,0:T(8,128)(2,1)S(1)} %copy-done.3, bf16[512,512]{1,0:T(8,128)(2,1)S(1)} %copy-done.4, ...), custom_call_target="tpu_custom_call" | custom-call | tf_op jit(solution)/shard_map/pallas_call | solution.py:395
  132.7 0.8 copy.15
  133.5 0.8 copy.16
  134.3 0.6 copy.17
Async XLA Ops:
  0.6 0.9 copy-start.5
  0.6 1.1 copy-start.3
  1.7 1.1 copy-start
  2.8 1.1 copy-start.1
  4.0 1.1 copy-start.2
  5.1 1.0 copy-start.4

commit v2 on v1

v2 whole, which is shorter than its diff:
```python
import jax
import jax.numpy as jnp
from jax import lax
from jax.experimental import pallas as pl
from jax.experimental.pallas import tpu as pltpu
from jax.sharding import PartitionSpec as P

CAP = 48
MESH = pl.DeviceIdType.MESH
F32 = jnp.float32
BF16 = jnp.bfloat16
NT = (((1,), (1,)), ((), ()))
ANTI = 7


def dot(a, b):
    return jnp.dot(a, b, preferred_element_type=F32)


def dot_nt(a, b):
    return lax.dot_general(a, b, NT, preferred_element_type=F32)


def kernel(
    routes, gates, tok_hbm, grad_hbm, wg_hbm, wu_hbm, wd_hbm,
    mixed, grad_tokens, grad_gates_t,
    rows_in, wg, wu, wd, ag, picked, sums, act, scl, hid, gg, gu, pb, rs_rx, rs_tx,
    ret, ret_tx, pick_t, wm_t, wm, xs_tx, xs_rx, zacc, zs_tx, zs_rx,
    g_tx, g_rx, g_all,
    w_sem, in_sem, ag_s, ag_r, rs_s, rs_r, pk_s, pk_r, rt_s, rt_r,
    xs_s, xs_r, zs_s, zs_r, za_s, za_r, xa_s, xa_r, g1_s, g1_r, g2_s, g2_r, g3_s, g3_r,
):
    y, t, e = lax.axis_index("dp"), lax.axis_index("tensor"), lax.axis_index("expert")
    n_dp = 8
    zh, core = t // 2, t % 2
    x, zl = e // 4, e % 4
    mirror = x * 4 + 3 - zl
    t1 = 2 * zh + 1 - core
    t2 = 2 * (1 - zh) + core
    t3 = 2 * (1 - zh) + 1 - core
    feats = (t, t1, t2, t3)
    experts = (4 * e + t, 4 * e + t1, 4 * mirror + t2, 4 * mirror + t3)
    peers = (None, (y, t1, e), (y, t2, mirror), (y, t3, mirror))
    up = (lax.rem(y + 1, n_dp), t, e)
    down = (lax.rem(y + n_dp - 1, n_dp), t, e)
    ring = (up, down)
    x_at = [lax.rem(x + rel, 4) for rel in range(4)]
    z_at = [lax.rem(zl + rel, 4) for rel in range(4)]
    x_peers = [(y, t, x_at[rel] * 4 + zl) for rel in range(4)]
    z_peers = [(y, t, x * 4 + z_at[rel]) for rel in range(4)]
    results = (mixed, grad_tokens)

    started = []

    def send(src, dst, s, r, to):
        copy = pltpu.make_async_remote_copy(
            src_ref=src, dst_ref=dst, send_sem=s, recv_sem=r, device_id=to, device_id_type=MESH
        )
        copy.start()
        started.append(copy)
        return copy

    barrier = pltpu.get_barrier_semaphore()
    everyone = list(ring) + list(peers[1:]) + x_peers[1:] + z_peers[1:]
    for peer in everyone:
        pl.semaphore_signal(barrier, inc=1, device_id=peer, device_id_type=MESH)

    row_loads = []
    for kind, hbm in enumerate((tok_hbm, grad_hbm)):
        load = pltpu.make_async_copy(hbm, rows_in.at[kind], in_sem.at[kind])
        load.start()
        row_loads.append(load)

    loads = []
    for n, (hbm, vmem) in enumerate(((wg_hbm, wg), (wu_hbm, wu), (wd_hbm, wd))):
        for j in range(4):
            at = pl.multiple_of(feats[j] * 512, 512)
            load = pltpu.make_async_copy(hbm.at[0, :, pl.ds(at, 512)], vmem.at[j], w_sem.at[n, j])
            load.start()
            loads.append(load)

    ids = routes[...]
    gate_rows = gates[...]
    row8 = lax.broadcasted_iota(jnp.int32, (8, 512), 0)
    masks = []
    chosen = jnp.zeros((8, 512), F32)
    for q in range(4):
        mask = jnp.sum((ids == experts[q]).astype(F32), axis=0, keepdims=True)
        masks.append(mask)
        chosen = chosen + jnp.where(row8 == q, mask, 0.0)
    rows512 = lax.broadcasted_iota(jnp.int32, (512, 512), 0)
    cols512 = lax.broadcasted_iota(jnp.int32, (512, 512), 1)
    before = (rows512 < cols512).astype(F32).astype(BF16)
    rank = dot(chosen.astype(BF16), before).astype(jnp.int32)
    slot = lax.broadcasted_iota(jnp.int32, (CAP, 512), 0)
    for q in range(4):
        hit = (slot == rank[q : q + 1]) & (masks[q] > 0.0)
        gate = jnp.sum(jnp.where(ids == experts[q], gate_rows, 0.0), axis=0, keepdims=True)
        pick_t[48 * q : 48 * q + 48] = jnp.where(hit, 1.0, 0.0).astype(BF16)
        wm_t[48 * q : 48 * q + 48] = jnp.where(hit, gate, 0.0).astype(BF16)

    ag_copy, pk_copy = {}, {}

    def ag_send(kind, way, d, j, src, dst):
        ag_copy[kind, way, d, j] = send(
            ag.at[kind, j, src], ag.at[kind, j, dst],
            ag_s.at[kind, way, d, j], ag_r.at[kind, way, d, j], ring[way],
        )

    def send_own(kind, j):
        ag_send(kind, 0, 0, j, 0, 1)
        ag_send(kind, 1, 0, j, 0, 2)

    for kind in range(2):
        row_loads[kind].wait()
        got = dot(pick_t[...], rows_in[kind]).astype(BF16)
        ag[kind, 0, 0] = got[0:48]
        for q in (2, 3, 1):
            picked[kind, q - 1] = got[48 * q : 48 * q + 48]
        if kind == 0:
            pl.semaphore_wait(barrier, len(everyone))
        for q in (1, 2, 3):
            pk_copy[kind, q] = send(
                picked.at[kind, q - 1], ag.at[kind, q, 0], pk_s.at[kind, q - 1], pk_r.at[kind, q - 1], peers[q]
            )
        send_own(kind, 0)

    def own_in(kind, j):
        pk_copy[kind, j].wait_recv()
        send_own(kind, j)

    own_in(0, 1)
    own_in(1, 1)
    for load in loads:
        load.wait()

    def rows_of(kind, j, s0, n):
        return ag[kind, j, s0 : s0 + n].reshape(n * CAP, 512)

    def half_sum(kind, w, j, s0, n):
        both = dot_nt(rows_of(kind, j, s0, n), w[j]) + dot_nt(rows_of(kind, j + 1, s0, n), w[j + 1])
        return both.reshape(n, CAP, 192)

    urgent, later = [], []

    def early(s0, n):
        def one(i, kind, w):
            sums[i, s0 : s0 + n] = half_sum(kind, w, 0, s0, n)

        return [lambda i=i, k=k, w=w: one(i, k, w) for i, (k, w) in enumerate(((0, wg), (0, wu), (1, wd)))]

    def forward(s0, n):
        def first():
            gate_pre = sums[0, s0 : s0 + n] + half_sum(0, wg, 2, s0, n)
            sig = jax.nn.sigmoid(gate_pre)
            act[s0 : s0 + n] = gate_pre * sig
            scl[s0 : s0 + n] = sig * (1.0 + gate_pre * (1.0 - sig))

        def second():
            up_pre = sums[1, s0 : s0 + n] + half_sum(0, wu, 2, s0, n)
            hid[s0 : s0 + n] = (act[s0 : s0 + n] * up_pre).astype(BF16)
            scl[s0 : s0 + n] = up_pre * scl[s0 : s0 + n]

        def third(j):
            out = dot(hid[s0 : s0 + n].reshape(n * CAP, 192), wd[j]).astype(BF16)
            for h in range(2):
                pb[0, h, s0 : s0 + n, j] = out[:, 256 * h : 256 * h + 256].reshape(n, CAP, 256)

        return [first, second] + [lambda j=j: third(j) for j in range(4)]

    def backward(s0, n):
        def first():
            grad_hid = sums[2, s0 : s0 + n] + half_sum(1, wd, 2, s0, n)
            gg[s0 : s0 + n] = (grad_hid * scl[s0 : s0 + n]).astype(BF16)
            gu[s0 : s0 + n] = (grad_hid * act[s0 : s0 + n]).astype(BF16)

        def second(j):
            back = dot(gg[s0 : s0 + n].reshape(n * CAP, 192), wg[j])
            back = back + dot(gu[s0 : s0 + n].reshape(n * CAP, 192), wu[j])
            back = back.astype(BF16)
            for h in range(2):
                pb[1, h, s0 : s0 + n, j] = back[:, 256 * h : 256 * h + 256].reshape(n, CAP, 256)

        return [first] + [lambda j=j: second(j) for j in range(4)]

    def work(n):
        for _ in range(min(n, len(urgent) + len(later))):
            (urgent or later).pop(0)()

    def span(d):
        return (2 * d - 1, 2) if d < 4 else (ANTI, 1)

    def arrive(kind, d, j):
        for way in range(2):
            if d == 4 and j % 2 != way:
                continue
            ag_copy[kind, way, d - 1, j].wait_recv()
            if d < 3:
                ag_send(kind, way, d, j, 2 * d - 1 + way, 2 * d + 1 + way)
            elif d == 3 and j % 2 == way:
                ag_send(kind, way, d, j, 2 * d - 1 + way, ANTI)

    urgent.extend(early(0, 1))
    for d in range(1, 5):
        for kind in range(2):
            for j in range(2):
                arrive(kind, d, j)
                work(1)
            if d == 4:
                own_in(kind, 2)
                own_in(kind, 3)
        urgent.extend(early(*span(d)))

    rs_copy = {}

    def rs_send(u, way, s, p, src):
        kind, h = u
        rs_copy[u, way, s, p] = send(
            src, rs_rx.at[kind, h, way, s, pl.ds(2 * p, 2)],
            rs_s.at[kind, h, way, s, p], rs_r.at[kind, h, way, s, p], ring[way],
        )

    def first(u):
        for way in range(2):
            rs_send(u, way, 0, way, pb.at[u[0], u[1], ANTI, pl.ds(2 * way, 2)])

    def free(u):
        for way in range(2):
            rs_send(u, way, 1, 1 - way, pb.at[u[0], u[1], 6 - way, pl.ds(2 - 2 * way, 2)])

    def add_on(u, s, turn):
        kind, h = u
        d = 4 - s
        for way in range(2):
            p = 1 - way if turn == 0 else way
            at, js = 2 * d - way, slice(2 * p, 2 * p + 2)
            rs_copy[u, way, s - 1, p].wait_recv()
            rs_tx[kind, h, way, s - 1, js] = (
                pb[kind, h, at, js].astype(F32) + rs_rx[kind, h, way, s - 1, js].astype(F32)
            ).astype(BF16)
        for way in range(2):
            p = 1 - way if turn == 0 else way
            rs_send(u, way, s, p, rs_tx.at[kind, h, way, s - 1, pl.ds(2 * p, 2)])

    def scatter(u, s):
        if s > 1:
            add_on(u, s, 0)
            work(2)
        add_on(u, s, 1)
        work(2)

    u0, u1, u2, u3 = (0, 0), (0, 1), (1, 0), (1, 1)

    urgent.extend(forward(0, 1))
    for d in range(1, 5):
        for j in (2, 3):
            arrive(0, d, j)
            work(4)
        if d == 1:
            later.extend(backward(0, 1))
        if d == 4:
            work(len(urgent))
            urgent.extend(forward(*span(d)))
            work(len(urgent))
            first(u0)
        else:
            urgent.extend(forward(*span(d)))
        for j in (2, 3):
            arrive(1, d, j)
            work(4)
        if d == 3:
            work(len(urgent))
            free(u0)
            free(u1)
        later.extend(backward(*span(d)))

    rt_copy, g_copy, e_copy = {}, {}, {}
    products = []

    def home(u):
        kind, h = u
        for p in (1, 0):
            for way in range(2):
                rs_copy[u, way, 3, p].wait_recv()
            for j in (2 * p + 1, 2 * p):
                total = (
                    pb[kind, h, 0, j].astype(F32)
                    + rs_rx[kind, h, 0, 3, j].astype(F32)
                    + rs_rx[kind, h, 1, 3, j].astype(F32)
                ).astype(BF16)
                if j == 0:
                    ret[kind, h, 0:48] = total
                else:
                    ret_tx[kind, h, j - 1] = total
                if kind == 0:
                    theirs = ag[1, j, 0, :, 256 * h : 256 * h + 256].astype(F32)
                    products.append(jnp.sum(total.astype(F32) * theirs, axis=1, keepdims=True))
            for j in (2 * p + 1, 2 * p):
                if j:
                    rt_copy[u, j] = send(
                        ret_tx.at[kind, h, j - 1], ret.at[kind, h, pl.ds(48 * j, 48)],
                        rt_s.at[kind, h, j - 1], rt_r.at[kind, h, j - 1], peers[j],
                    )

    def gates_first():
        total = products[0]
        for term in products[1:]:
            total = total + term
        own = jnp.sum(pick_t[0:48].astype(F32) * total, axis=0, keepdims=True)
        g_tx[0] = jnp.broadcast_to(own, (8, 512))
        for j in (2, 3, 1):
            g_copy[1, j] = send(g_tx.at[0], g_rx.at[j - 1], g1_s.at[j - 1], g1_r.at[j - 1], peers[j])

    def gates_second():
        block = jnp.where(row8 == 0, g_tx[0], 0.0)
        for j in range(1, 4):
            g_copy[1, j].wait_recv()
            block = block + jnp.where(row8 == j, g_rx[j - 1], 0.0)
        g_tx[1] = block
        g_all[zl, x] = block
        for rel in range(1, 4):
            g_copy[2, rel] = send(
                g_tx.at[1], g_all.at[zl, x], g2_s.at[rel - 1], g2_r.at[rel - 1], x_peers[rel]
            )

    def gates_third():
        for rel in range(1, 4):
            g_copy[2, rel].wait_recv()
        for rel in range(1, 4):
            g_copy[3, rel] = send(
                g_all.at[zl], g_all.at[zl], g3_s.at[rel - 1], g3_r.at[rel - 1], z_peers[rel]
            )

    def gates_last():
        for rel in range(1, 4):
            g_copy[3, rel].wait_recv()
        ids_now = routes[...]
        totals = [jnp.zeros((8, 512), F32) for _ in range(8)]
        for zz in range(4):
            for xx in range(4):
                there, opposite = 4 * (xx * 4 + zz), 4 * (xx * 4 + 3 - zz)
                names = jnp.where(row8 == 0, there + t, -1)
                names = jnp.where(row8 == 1, there + t1, names)
                names = jnp.where(row8 == 2, opposite + t2, names)
                names = jnp.where(row8 == 3, opposite + t3, names)
                block = g_all[zz, xx]
                for r in range(8):
                    totals[r] = totals[r] + jnp.where(ids_now[r : r + 1] == names, block, 0.0)
        for r in range(8):
            grad_gates_t[r : r + 1] = jnp.sum(totals[r], axis=0, keepdims=True)

    def x_scatter(u):
        kind, h = u
        for j in (1, 2, 3):
            rt_copy[u, j].wait_recv()
        for rel in (2, 1, 3):
            rows = pl.ds(pl.multiple_of(x_at[rel] * 128, 128), 128)
            xs_tx[kind, h, rel - 1] = dot(wm[rows], ret[kind, h]).astype(BF16)
            e_copy["xs", u, rel] = send(
                xs_tx.at[kind, h, rel - 1], xs_rx.at[kind, h, rel - 1],
                xs_s.at[kind, h, rel - 1], xs_r.at[kind, h, rel - 1], x_peers[rel],
            )
        zacc[kind, h] = dot(wm[pl.ds(pl.multiple_of(x * 128, 128), 128)], ret[kind, h])

    def z_scatter(u):
        kind, h = u
        for rel in (1, 3, 2):
            e_copy["xs", u, rel].wait_recv()
        total = zacc[kind, h]
        for rel in range(1, 4):
            total = total + xs_rx[kind, h, rel - 1].astype(F32)
        zacc[kind, h] = total
        zs_tx[kind, h] = total.astype(BF16)
        for rel in (2, 1, 3):
            rows = pl.ds(pl.multiple_of(z_at[rel] * 32, 32), 32)
            e_copy["zs", u, rel] = send(
                zs_tx.at[kind, h, rows], zs_rx.at[kind, h, rel - 1],
                zs_s.at[kind, h, rel - 1], zs_r.at[kind, h, rel - 1], z_peers[rel],
            )

    def z_gather(u):
        kind, h = u
        total = zacc[kind, h, pl.ds(pl.multiple_of(zl * 32, 32), 32)]
        for rel in (1, 3, 2):
            e_copy["zs", u, rel].wait_recv()
        for rel in range(1, 4):
            total = total + zs_rx[kind, h, rel - 1].astype(F32)
        rows = pl.ds(pl.multiple_of(x * 128 + zl * 32, 32), 32)
        out = results[kind]
        out[rows, 256 * h : 256 * h + 256] = total.astype(BF16)
        place = out.at[rows, pl.ds(256 * h, 256)]
        for rel in (2, 1, 3):
            e_copy["za", u, rel] = send(
                place, place, za_s.at[kind, h, rel - 1], za_r.at[kind, h, rel - 1], z_peers[rel]
            )

    def x_gather(u):
        kind, h = u
        for rel in (1, 3, 2):
            e_copy["za", u, rel].wait_recv()
        rows = pl.ds(pl.multiple_of(x * 128, 128), 128)
        place = results[kind].at[rows, pl.ds(256 * h, 256)]
        for rel in (2, 1, 3):
            e_copy["xa", u, rel] = send(
                place, place, xa_s.at[kind, h, rel - 1], xa_r.at[kind, h, rel - 1], x_peers[rel]
            )

    def finish(u):
        for rel in (1, 3, 2):
            e_copy["xa", u, rel].wait_recv()

    wm[...] = dot_nt((rows512 == cols512).astype(F32).astype(BF16), wm_t[...]).astype(BF16)
    first(u1)
    scatter(u0, 1)
    scatter(u1, 1)
    scatter(u0, 2)
    work(len(urgent) + len(later))
    free(u2)
    free(u3)
    scatter(u0, 3)
    first(u2)
    scatter(u1, 2)
    home(u0)
    scatter(u1, 3)
    scatter(u2, 1)
    x_scatter(u0)
    first(u3)
    scatter(u2, 2)
    home(u1)
    scatter(u2, 3)
    gates_first()
    scatter(u3, 1)
    z_scatter(u0)
    x_scatter(u1)
    scatter(u3, 2)
    z_gather(u0)
    home(u2)
    scatter(u3, 3)
    gates_second()
    z_scatter(u1)
    x_scatter(u2)
    x_gather(u0)
    home(u3)
    gates_third()
    z_gather(u1)
    z_scatter(u2)
    x_scatter(u3)
    x_gather(u1)
    z_gather(u2)
    gates_last()
    z_scatter(u3)
    x_gather(u2)
    z_gather(u3)
    x_gather(u3)
    for u in (u0, u1, u2, u3):
        finish(u)
    for copy in started:
        copy.wait_send()


def body(tokens, grad_out, routes, gates, gate_weight, up_weight, down_weight):
    vmem = pl.BlockSpec(memory_space=pltpu.VMEM)
    hbm = pl.BlockSpec(memory_space=pltpu.HBM)
    dma = pltpu.SemaphoreType.DMA
    mixed, grad_tokens, grad_gates_t = pl.pallas_call(
        kernel,
        out_shape=(
            jax.ShapeDtypeStruct((512, 512), BF16),
            jax.ShapeDtypeStruct((512, 512), BF16),
            jax.ShapeDtypeStruct((8, 512), F32),
        ),
        in_specs=[vmem] * 2 + [hbm] * 5,
        out_specs=(vmem, vmem, vmem),
        scratch_shapes=[
            pltpu.VMEM((2, 512, 512), BF16),
            pltpu.VMEM((4, 192, 512), BF16),
            pltpu.VMEM((4, 192, 512), BF16),
            pltpu.VMEM((4, 192, 512), BF16),
            pltpu.VMEM((2, 4, 8, CAP, 512), BF16),
            pltpu.VMEM((2, 3, CAP, 512), BF16),
            pltpu.VMEM((3, 8, CAP, 192), F32),
            pltpu.VMEM((8, CAP, 192), F32),
            pltpu.VMEM((8, CAP, 192), F32),
            pltpu.VMEM((8, CAP, 192), BF16),
            pltpu.VMEM((8, CAP, 192), BF16),
            pltpu.VMEM((8, CAP, 192), BF16),
            pltpu.VMEM((2, 2, 8, 4, CAP, 256), BF16),
            pltpu.VMEM((2, 2, 2, 4, 4, CAP, 256), BF16),
            pltpu.VMEM((2, 2, 2, 3, 4, CAP, 256), BF16),
            pltpu.VMEM((2, 2, 192, 256), BF16),
            pltpu.VMEM((2, 2, 3, CAP, 256), BF16),
            pltpu.VMEM((192, 512), BF16),
            pltpu.VMEM((192, 512), BF16),
            pltpu.VMEM((512, 192), BF16),
            pltpu.VMEM((2, 2, 3, 128, 256), BF16),
            pltpu.VMEM((2, 2, 3, 128, 256), BF16),
            pltpu.VMEM((2, 2, 128, 256), F32),
            pltpu.VMEM((2, 2, 128, 256), BF16),
            pltpu.VMEM((2, 2, 3, 32, 256), BF16),
            pltpu.VMEM((2, 8, 512), F32),
            pltpu.VMEM((3, 8, 512), F32),
            pltpu.VMEM((4, 4, 8, 512), F32),
            dma((3, 4)),
            dma((2,)),
            dma((2, 2, 4, 4)),
            dma((2, 2, 4, 4)),
            dma((2, 2, 2, 4, 2)),
            dma((2, 2, 2, 4, 2)),
            dma((2, 3)),
            dma((2, 3)),
        ]
        + [dma((2, 2, 3))] * 10
        + [dma((3,))] * 6,
        compiler_params=pltpu.CompilerParams(
            collective_id=0, has_side_effects=True, vmem_limit_bytes=60500000
        ),
    )(routes.T, gates.T, tokens, grad_out, gate_weight, up_weight, down_weight)
    return mixed, grad_tokens, grad_gates_t.T


def solution(mesh):
    return jax.shard_map(
        body,
        mesh=mesh,
        in_specs=(
            P("dp", "tensor"),
            P("dp", "tensor"),
            P("dp", None),
            P("dp", None),
            P(("expert", "tensor"), "dp", None),
            P(("expert", "tensor"), "dp", None),
            P(("expert", "tensor"), "dp", None),
        ),
        out_specs=(P("dp", "tensor"), P("dp", "tensor"), P("dp", None)),
        check_vma=False,
    )
```

time: 135 us -> 120 us (0.89)
  the two profiles are of different devices: /device:TPU:16 before, /device:TPU:24 now
where the time goes in v2:
time: 120 us; the launch traced here: 119 us
  Pallas kernels  115 us (96%)
  local copies, waits for them, and re-layouts  3.33 us (3%)
    pallas_call x1, Pallas kernels, body(): pl.pallas_call(kernel, out_shape=(jax.ShapeDtypeStruct((512, 512), BF16),...  115 us
    unnamed x7, local copies, waits for them, and re-layouts  3.33 us

profile of v2, /device:TPU:24, one launch (start us, length us, event | category | flops | bytes accessed | tf_op | source)
XLA Modules:
  0.0 119.4 jit_solution(15502532796389330177)
XLA Ops:
  0.6 115.4 %shard_map.94 = (bf16[512,512]{1,0:T(8,128)(2,1)}, bf16[512,512]{1,0:T(8,128)(2,1)}, f32[8,512]{1,0:T(8,128)}) custom-call(s32[8,512]{1,0:T(8,128)} %bitcast.3, f32[8,512]{1,0:T(8,128)} %bitcast.4, bf16[512,512]{1,0:T(8,128)(2,1)} %tok_hbm.1, bf16[512,512]{1,0:T(8,128)(2,1)} %grad_hbm.1, bf16[1,192,2048]{2,1,0:T(8,128)(2,1)} %wg_hbm.1, ...), custom_call_target="tpu_custom_call" | custom-call | tf_op jit(solution)/shard_map/pallas_call | solution.py:465
  116.0 0.0 copy-start
  116.0 1.9 %copy.13 = bf16[512,512]{1,0:T(8,128)(2,1)} copy(bf16[512,512]{1,0:T(8,128)(2,1)} %get-tuple-element.12) | data formatting | bytes 1048576
  118.0 0.0 copy-done
  118.0 0.0 copy-start.1
  118.0 0.8 copy.14
  118.8 0.0 copy-done.1
  118.8 0.6 copy.15
Async XLA Ops:
  116.0 1.9 %copy-start = (bf16[512,512]{1,0:T(8,128)(2,1)S(1)}, bf16[512,512]{1,0:T(8,128)(2,1)}, u32[]{:S(2)}) copy-start(bf16[512,512]{1,0:T(8,128)(2,1)} %get-tuple-element.13) | copy-start | bytes 1572868
  118.0 0.8 copy-start.1

commit v3 on v2

v3 whole, which is shorter than its diff:
```python
import jax
import jax.numpy as jnp
from jax import lax
from jax.experimental import pallas as pl
from jax.experimental.pallas import tpu as pltpu
from jax.sharding import PartitionSpec as P

CAP = 48
MESH = pl.DeviceIdType.MESH
F32 = jnp.float32
BF16 = jnp.bfloat16
NT = (((1,), (1,)), ((), ()))
ANTI = 7
UNITS = ((0, 0, 0, 256), (0, 1, 0, 256), (1, 0, 0, 256), (1, 1, 0, 128), (1, 1, 128, 128))
PLAN = (
    ("ag", 0, 0, 1), ("E", 0, 0), ("E", 1, 0), ("ag", 0, 1, 0), ("ag", 1, 0, 1), ("E", 2, 0),
    ("ag", 1, 1, 0), ("ag", 0, 1, 1), ("E", 0, 1), ("E", 1, 1), ("ag", 0, 2, 0), ("ag", 0, 0, 2),
    ("F", 0), ("ag", 0, 0, 3), ("G", 0), ("P", 0, 0, 0), ("P", 0, 0, 1), ("P", 0, 0, 2),
    ("ag", 1, 1, 1), ("P", 0, 0, 3), ("E", 2, 1), ("E", 0, 2), ("ag", 0, 2, 1), ("E", 1, 2),
    ("ag", 0, 3, 0), ("B", 0), ("P", 1, 0, 0), ("ag", 1, 0, 2), ("P", 1, 0, 1), ("P", 1, 0, 2),
    ("P", 1, 0, 3), ("ag", 0, 1, 2), ("F", 1), ("G", 1), ("P", 0, 1, 0), ("ag", 0, 1, 3),
    ("P", 0, 1, 1), ("P", 0, 1, 2), ("P", 0, 1, 3), ("E", 2, 2), ("ag", 1, 0, 3), ("E", 0, 3),
    ("E", 1, 3), ("ag", 0, 3, 1), ("ag", 1, 2, 0), ("ag", 1, 1, 2), ("ag", 0, 2, 2), ("F", 2),
    ("G", 2), ("P", 0, 2, 0), ("ag", 0, 2, 3), ("P", 0, 2, 1), ("P", 0, 2, 2), ("P", 0, 2, 3),
    ("E", 0, 4), ("ag", 1, 1, 3), ("E", 1, 4), ("B", 1), ("P", 1, 1, 0), ("ag", 1, 2, 1),
    ("P", 1, 1, 1), ("P", 1, 1, 2), ("P", 1, 1, 3), ("ag", 1, 2, 2), ("ag", 0, 3, 2),
    ("ag", 1, 3, 0), ("F", 3), ("ag", 0, 3, 3), ("G", 3), ("P", 0, 3, 0), ("P", 0, 3, 1),
    ("ag", 1, 2, 3), ("P", 0, 3, 2), ("P", 0, 3, 3), ("free", 0), ("B", 2), ("E", 2, 3),
    ("P", 1, 2, 0), ("P", 1, 2, 1), ("free", 1), ("P", 1, 2, 2), ("P", 1, 2, 3), ("ag", 1, 3, 1),
    ("ag", 1, 3, 2), ("F", 4), ("G", 4), ("P", 0, 4, 0), ("P", 0, 4, 1), ("ag", 1, 3, 3),
    ("P", 0, 4, 2), ("P", 0, 4, 3), ("wm",), ("first", 0), ("first", 1), ("B", 3), ("P", 1, 3, 0),
    ("P", 1, 3, 1), ("short", 0, 2), ("P", 1, 3, 2), ("P", 1, 3, 3), ("E", 2, 4), ("free", 2),
    ("B", 4), ("free", 3), ("P", 1, 4, 0), ("P", 1, 4, 1), ("free", 4), ("P", 1, 4, 2),
    ("long", 0, 1), ("P", 1, 4, 3), ("first", 2), ("short", 0, 3), ("short", 2, 2), ("first", 3),
    ("short", 3, 2), ("long", 0, 2), ("long", 2, 1), ("first", 4), ("short", 4, 2), ("short", 2, 3),
    ("long", 3, 1), ("short", 3, 3), ("long", 0, 3), ("long", 2, 2), ("long", 4, 1),
    ("short", 4, 3), ("long", 1, 1), ("long", 3, 2), ("short", 1, 2), ("home", 0), ("long", 2, 3),
    ("long", 4, 2), ("long", 1, 2), ("long", 3, 3), ("xs", 0), ("short", 1, 3), ("home", 2),
    ("long", 4, 3), ("long", 1, 3), ("home", 3), ("home", 4), ("zs", 0), ("xs", 2), ("home", 1),
    ("g1",), ("xs", 3), ("zg", 0), ("xs", 4), ("g2",), ("xs", 1), ("zs", 2), ("xg", 0), ("zs", 3),
    ("g3",), ("zs", 4), ("zg", 2), ("zg", 3), ("zs", 1), ("g4",), ("zg", 4), ("xg", 2), ("fin", 0),
    ("xg", 3), ("zg", 1), ("xg", 4), ("fin", 2), ("xg", 1), ("fin", 3), ("fin", 4), ("fin", 1),
)


def dot(a, b):
    return jnp.dot(a, b, preferred_element_type=F32)


def dot_nt(a, b):
    return lax.dot_general(a, b, NT, preferred_element_type=F32)


def kernel(
    routes_hbm, gates_hbm, tok_hbm, grad_hbm, wg_hbm, wu_hbm, wd_hbm,
    mixed, grad_tokens, grad_gates_t,
    routes, gates, rows_in, wg, wu, wd, ag, picked, sums, act, scl, hid, gg, gu, pb, rs_rx, rs_tx,
    ret, ret_tx, pick_t, wm_t, wm, xs_tx, xs_rx, zacc, zs_tx, zs_rx,
    g_tx, g_rx,
    w_sem, in_sem, ag_s, ag_r, rs_s, rs_r, pk_s, pk_r, rt_s, rt_r,
    xs_s, xs_r, zs_s, zs_r, za_s, za_r, xa_s, xa_r, g_s, g_r,
):
    y, t, e = lax.axis_index("dp"), lax.axis_index("tensor"), lax.axis_index("expert")
    n_dp = 8
    zh, core = t // 2, t % 2
    x, zl = e // 4, e % 4
    mirror = x * 4 + 3 - zl
    t1 = 2 * zh + 1 - core
    t2 = 2 * (1 - zh) + core
    t3 = 2 * (1 - zh) + 1 - core
    feats = (t, t1, t2, t3)
    experts = (4 * e + t, 4 * e + t1, 4 * mirror + t2, 4 * mirror + t3)
    peers = (None, (y, t1, e), (y, t2, mirror), (y, t3, mirror))
    up = (lax.rem(y + 1, n_dp), t, e)
    down = (lax.rem(y + n_dp - 1, n_dp), t, e)
    ring = (up, down)
    x_at = [lax.rem(x + rel, 4) for rel in range(4)]
    z_at = [lax.rem(zl + rel, 4) for rel in range(4)]
    x_peers = [(y, t, x_at[rel] * 4 + zl) for rel in range(4)]
    z_peers = [(y, t, x * 4 + z_at[rel]) for rel in range(4)]
    results = (mixed, grad_tokens)

    started = []

    def send(src, dst, s, r, to):
        copy = pltpu.make_async_remote_copy(
            src_ref=src, dst_ref=dst, send_sem=s, recv_sem=r, device_id=to, device_id_type=MESH
        )
        copy.start()
        started.append(copy)
        return copy

    barrier = pltpu.get_barrier_semaphore()
    everyone = list(ring) + list(peers[1:]) + x_peers[1:] + z_peers[1:]
    for peer in everyone:
        pl.semaphore_signal(barrier, inc=1, device_id=peer, device_id_type=MESH)

    row_loads = []
    route_loads = []
    for n, (hbm, vmem) in enumerate(((routes_hbm, routes), (gates_hbm, gates))):
        load = pltpu.make_async_copy(hbm, vmem, in_sem.at[2 + n])
        load.start()
        route_loads.append(load)
    for kind, hbm in enumerate((tok_hbm, grad_hbm)):
        load = pltpu.make_async_copy(hbm, rows_in.at[kind], in_sem.at[kind])
        load.start()
        row_loads.append(load)

    loads = [[], [], []]
    for n, (hbm, vmem) in enumerate(((wg_hbm, wg), (wu_hbm, wu), (wd_hbm, wd))):
        for j in range(4):
            at = pl.multiple_of(feats[j] * 512, 512)
            load = pltpu.make_async_copy(hbm.at[0, :, pl.ds(at, 512)], vmem.at[j], w_sem.at[n, j])
            load.start()
            loads[n].append(load)

    for load in route_loads:
        load.wait()
    ids = routes[...]
    gate_rows = gates[...]
    row8 = lax.broadcasted_iota(jnp.int32, (8, 512), 0)
    masks = []
    chosen = jnp.zeros((8, 512), F32)
    for q in range(4):
        mask = jnp.sum((ids == experts[q]).astype(F32), axis=0, keepdims=True)
        masks.append(mask)
        chosen = chosen + jnp.where(row8 == q, mask, 0.0)
    rows512 = lax.broadcasted_iota(jnp.int32, (512, 512), 0)
    cols512 = lax.broadcasted_iota(jnp.int32, (512, 512), 1)
    before = (rows512 < cols512).astype(F32).astype(BF16)
    rank = dot(chosen.astype(BF16), before).astype(jnp.int32)
    slot = lax.broadcasted_iota(jnp.int32, (CAP, 512), 0)
    for q in range(4):
        hit = (slot == rank[q : q + 1]) & (masks[q] > 0.0)
        gate = jnp.sum(jnp.where(ids == experts[q], gate_rows, 0.0), axis=0, keepdims=True)
        pick_t[48 * q : 48 * q + 48] = jnp.where(hit, 1.0, 0.0).astype(BF16)
        wm_t[48 * q : 48 * q + 48] = jnp.where(hit, gate, 0.0).astype(BF16)

    ag_copy, pk_copy = {}, {}

    def ag_send(kind, way, d, j, src, dst):
        ag_copy[kind, way, d, j] = send(
            ag.at[kind, j, src], ag.at[kind, j, dst],
            ag_s.at[kind, way, d, j], ag_r.at[kind, way, d, j], ring[way],
        )

    def send_own(kind, j):
        ag_send(kind, 0, 0, j, 0, 1)
        ag_send(kind, 1, 0, j, 0, 2)

    for kind in range(2):
        row_loads[kind].wait()
        got = dot(pick_t[...], rows_in[kind]).astype(BF16)
        ag[kind, 0, 0] = got[0:48]
        for q in (2, 3, 1):
            picked[kind, q - 1] = got[48 * q : 48 * q + 48]
        if kind == 0:
            pl.semaphore_wait(barrier, len(everyone))
        for q in (1, 2, 3):
            pk_copy[kind, q] = send(
                picked.at[kind, q - 1], ag.at[kind, q, 0], pk_s.at[kind, q - 1], pk_r.at[kind, q - 1], peers[q]
            )
        send_own(kind, 0)

    here = {(0, 0, 0), (1, 0, 0)}

    def arrived(kind, d, j):
        if (kind, d, j) in here:
            return
        here.add((kind, d, j))
        if d == 0:
            pk_copy[kind, j].wait_recv()
            return
        for way in range(2):
            if d < 4 or j % 2 == way:
                ag_copy[kind, way, d - 1, j].wait_recv()

    def rows_of(kind, j, s0, n):
        return ag[kind, j, s0 : s0 + n].reshape(n * CAP, 512)

    def half_sum(kind, w, j, s0, n):
        both = dot_nt(rows_of(kind, j, s0, n), w[j]) + dot_nt(rows_of(kind, j + 1, s0, n), w[j + 1])
        return both.reshape(n, CAP, 192)

    def span(d):
        return ((0, 1), (1, 2), (3, 2), (5, 2), (ANTI, 1))[d]

    def early(i, d):
        kind, w = ((0, wg), (0, wu), (1, wd))[i]
        while loads[i]:
            loads[i].pop().wait()
        arrived(kind, d, 0)
        arrived(kind, d, 1)
        s0, n = span(d)
        sums[i, s0 : s0 + n] = half_sum(kind, w, 0, s0, n)

    def activate(d):
        arrived(0, d, 2)
        arrived(0, d, 3)
        s0, n = span(d)
        gate_pre = sums[0, s0 : s0 + n] + half_sum(0, wg, 2, s0, n)
        sig = jax.nn.sigmoid(gate_pre)
        act[s0 : s0 + n] = gate_pre * sig
        scl[s0 : s0 + n] = sig * (1.0 + gate_pre * (1.0 - sig))

    def hide(d):
        s0, n = span(d)
        up_pre = sums[1, s0 : s0 + n] + half_sum(0, wu, 2, s0, n)
        hid[s0 : s0 + n] = (act[s0 : s0 + n] * up_pre).astype(BF16)
        scl[s0 : s0 + n] = up_pre * scl[s0 : s0 + n]

    def turn_back(d):
        arrived(1, d, 2)
        arrived(1, d, 3)
        s0, n = span(d)
        grad_hid = sums[2, s0 : s0 + n] + half_sum(1, wd, 2, s0, n)
        gg[s0 : s0 + n] = (grad_hid * scl[s0 : s0 + n]).astype(BF16)
        gu[s0 : s0 + n] = (grad_hid * act[s0 : s0 + n]).astype(BF16)

    def partial(kind, d, j):
        s0, n = span(d)
        if kind == 0:
            part = dot(hid[s0 : s0 + n].reshape(n * CAP, 192), wd[j])
        else:
            part = dot(gg[s0 : s0 + n].reshape(n * CAP, 192), wg[j])
            part = part + dot(gu[s0 : s0 + n].reshape(n * CAP, 192), wu[j])
        part = part.astype(BF16)
        for h in range(2):
            pb[kind, h, s0 : s0 + n, j] = part[:, 256 * h : 256 * h + 256].reshape(n, CAP, 256)

    def gather(kind, d, j):
        arrived(kind, d, j)
        if d == 0:
            send_own(kind, j)
            return
        for way in range(2):
            if d < 3:
                ag_send(kind, way, d, j, 2 * d - 1 + way, 2 * d + 1 + way)
            elif j % 2 == way:
                ag_send(kind, way, d, j, 2 * d - 1 + way, ANTI)

    rs_copy = {}

    def rs_send(u, way, s, p, src):
        kind, h, o, w = UNITS[u]
        rs_copy[u, way, s, p] = send(
            src, rs_rx.at[kind, h, way, s, pl.ds(2 * p, 2), :, pl.ds(o, w)],
            rs_s.at[u, way, s, p], rs_r.at[u, way, s, p], ring[way],
        )

    def first(u):
        kind, h, o, w = UNITS[u]
        for way in range(2):
            rs_send(u, way, 0, way, pb.at[kind, h, ANTI, pl.ds(2 * way, 2), :, pl.ds(o, w)])

    def free(u):
        kind, h, o, w = UNITS[u]
        for way in range(2):
            rs_send(u, way, 1, 1 - way, pb.at[kind, h, 6 - way, pl.ds(2 - 2 * way, 2), :, pl.ds(o, w)])

    def add_on(u, s, turn):
        kind, h, o, w = UNITS[u]
        for way in range(2):
            p = 1 - way if turn == 0 else way
            at, js = 8 - 2 * s - way, slice(2 * p, 2 * p + 2)
            rs_copy[u, way, s - 1, p].wait_recv()
            rs_tx[kind, h, way, s - 1, js, :, o : o + w] = (
                pb[kind, h, at, js, :, o : o + w].astype(F32)
                + rs_rx[kind, h, way, s - 1, js, :, o : o + w].astype(F32)
            ).astype(BF16)
        for way in range(2):
            p = 1 - way if turn == 0 else way
            src = rs_tx.at[kind, h, way, s - 1, pl.ds(2 * p, 2), :, pl.ds(o, w)]
            rs_send(u, way, s, p, src)

    def long(u, s):
        add_on(u, s, 1)

    def short(u, s):
        add_on(u, s, 0)

    rt_copy, g_copy, e_copy = {}, {}, {}
    products = []

    def home(u):
        kind, h, o, w = UNITS[u]
        lanes = slice(o, o + w)
        for p in (1, 0):
            for way in range(2):
                rs_copy[u, way, 3, p].wait_recv()
            for j in (2 * p + 1, 2 * p):
                total = (
                    pb[kind, h, 0, j, :, lanes].astype(F32)
                    + rs_rx[kind, h, 0, 3, j, :, lanes].astype(F32)
                    + rs_rx[kind, h, 1, 3, j, :, lanes].astype(F32)
                ).astype(BF16)
                if j == 0:
                    ret[kind, h, 0:48, lanes] = total
                else:
                    ret_tx[kind, h, j - 1, :, lanes] = total
                if kind == 0:
                    theirs = ag[1, j, 0, :, 256 * h : 256 * h + 256].astype(F32)
                    products.append(jnp.sum(total.astype(F32) * theirs, axis=1, keepdims=True))
            for j in (2 * p + 1, 2 * p):
                if j:
                    rt_copy[u, j] = send(
                        ret_tx.at[kind, h, j - 1, :, pl.ds(o, w)],
                        ret.at[kind, h, pl.ds(48 * j, 48), pl.ds(o, w)],
                        rt_s.at[u, j - 1], rt_r.at[u, j - 1], peers[j],
                    )

    def gates_send(stage, block, to):
        g_tx[stage] = block
        for i in range(3):
            g_copy[stage, i] = send(
                g_tx.at[stage], g_rx.at[stage, i], g_s.at[stage, i], g_r.at[stage, i], to[i + 1]
            )

    def gates_sum(stage):
        block = g_tx[stage]
        for i in range(3):
            g_copy[stage, i].wait_recv()
            block = block + g_rx[stage, i]
        return block

    def gates_first():
        total = products[0]
        for term in products[1:]:
            total = total + term
        own = jnp.sum(pick_t[0:48].astype(F32) * total, axis=0, keepdims=True)
        gates_send(0, jnp.where(routes[...] == experts[0], own, 0.0), peers)

    def gates_second():
        gates_send(1, gates_sum(0), x_peers)

    def gates_third():
        gates_send(2, gates_sum(1), z_peers)

    def gates_last():
        grad_gates_t[...] = gates_sum(2)

    def x_scatter(u):
        kind, h, o, w = UNITS[u]
        for j in (1, 2, 3):
            rt_copy[u, j].wait_recv()
        slots = ret[kind, h, :, o : o + w]
        for rel in (2, 1, 3):
            rows = pl.ds(pl.multiple_of(x_at[rel] * 128, 128), 128)
            xs_tx[kind, h, rel - 1, :, o : o + w] = dot(wm[rows], slots).astype(BF16)
        for rel in (2, 1, 3):
            e_copy["xs", u, rel] = send(
                xs_tx.at[kind, h, rel - 1, :, pl.ds(o, w)], xs_rx.at[kind, h, rel - 1, :, pl.ds(o, w)],
                xs_s.at[u, rel - 1], xs_r.at[u, rel - 1], x_peers[rel],
            )
        zacc[kind, h, :, o : o + w] = dot(wm[pl.ds(pl.multiple_of(x * 128, 128), 128)], slots)

    def z_scatter(u):
        kind, h, o, w = UNITS[u]
        for rel in (1, 3, 2):
            e_copy["xs", u, rel].wait_recv()
        total = zacc[kind, h, :, o : o + w]
        for rel in range(1, 4):
            total = total + xs_rx[kind, h, rel - 1, :, o : o + w].astype(F32)
        zacc[kind, h, :, o : o + w] = total
        zs_tx[kind, h, :, o : o + w] = total.astype(BF16)
        for rel in (2, 1, 3):
            rows = pl.ds(pl.multiple_of(z_at[rel] * 32, 32), 32)
            e_copy["zs", u, rel] = send(
                zs_tx.at[kind, h, rows, pl.ds(o, w)], zs_rx.at[kind, h, rel - 1, :, pl.ds(o, w)],
                zs_s.at[u, rel - 1], zs_r.at[u, rel - 1], z_peers[rel],
            )

    def z_gather(u):
        kind, h, o, w = UNITS[u]
        total = zacc[kind, h, pl.ds(pl.multiple_of(zl * 32, 32), 32), o : o + w]
        for rel in (1, 3, 2):
            e_copy["zs", u, rel].wait_recv()
        for rel in range(1, 4):
            total = total + zs_rx[kind, h, rel - 1, :, o : o + w].astype(F32)
        rows = pl.ds(pl.multiple_of(x * 128 + zl * 32, 32), 32)
        out = results[kind]
        out[rows, 256 * h + o : 256 * h + o + w] = total.astype(BF16)
        place = out.at[rows, pl.ds(256 * h + o, w)]
        for rel in (2, 1, 3):
            e_copy["za", u, rel] = send(place, place, za_s.at[u, rel - 1], za_r.at[u, rel - 1], z_peers[rel])

    def x_gather(u):
        kind, h, o, w = UNITS[u]
        for rel in (1, 3, 2):
            e_copy["za", u, rel].wait_recv()
        rows = pl.ds(pl.multiple_of(x * 128, 128), 128)
        place = results[kind].at[rows, pl.ds(256 * h + o, w)]
        for rel in (2, 1, 3):
            e_copy["xa", u, rel] = send(place, place, xa_s.at[u, rel - 1], xa_r.at[u, rel - 1], x_peers[rel])

    def finish(u):
        for rel in (1, 3, 2):
            e_copy["xa", u, rel].wait_recv()

    def weigh():
        wm[...] = dot_nt((rows512 == cols512).astype(F32).astype(BF16), wm_t[...]).astype(BF16)

    steps = {
        "ag": gather, "E": early, "F": activate, "G": hide, "B": turn_back, "P": partial,
        "first": first, "free": free, "long": long, "short": short, "home": home,
        "xs": x_scatter, "zs": z_scatter, "zg": z_gather, "xg": x_gather, "fin": finish,
        "g1": gates_first, "g2": gates_second, "g3": gates_third, "g4": gates_last, "wm": weigh,
    }
    for name, *at in PLAN:
        steps[name](*at)
    for copy in started:
        copy.wait_send()


def body(tokens, grad_out, routes, gates, gate_weight, up_weight, down_weight):
    vmem = pl.BlockSpec(memory_space=pltpu.VMEM)
    hbm = pl.BlockSpec(memory_space=pltpu.HBM)
    dma = pltpu.SemaphoreType.DMA
    operands = (routes.T, gates.T, tokens, grad_out, gate_weight, up_weight, down_weight)
    mixed, grad_tokens, grad_gates_t = pl.pallas_call(
        kernel,
        out_shape=(
            jax.ShapeDtypeStruct((512, 512), BF16),
            jax.ShapeDtypeStruct((512, 512), BF16),
            jax.ShapeDtypeStruct((8, 512), F32),
        ),
        in_specs=[hbm] * 7,
        out_specs=(vmem, vmem, vmem),
        scratch_shapes=[
            pltpu.VMEM((8, 512), jnp.int32),
            pltpu.VMEM((8, 512), F32),
            pltpu.VMEM((2, 512, 512), BF16),
            pltpu.VMEM((4, 192, 512), BF16),
            pltpu.VMEM((4, 192, 512), BF16),
            pltpu.VMEM((4, 192, 512), BF16),
            pltpu.VMEM((2, 4, 8, CAP, 512), BF16),
            pltpu.VMEM((2, 3, CAP, 512), BF16),
            pltpu.VMEM((3, 8, CAP, 192), F32),
            pltpu.VMEM((8, CAP, 192), F32),
            pltpu.VMEM((8, CAP, 192), F32),
            pltpu.VMEM((8, CAP, 192), BF16),
            pltpu.VMEM((8, CAP, 192), BF16),
            pltpu.VMEM((8, CAP, 192), BF16),
            pltpu.VMEM((2, 2, 8, 4, CAP, 256), BF16),
            pltpu.VMEM((2, 2, 2, 4, 4, CAP, 256), BF16),
            pltpu.VMEM((2, 2, 2, 3, 4, CAP, 256), BF16),
            pltpu.VMEM((2, 2, 192, 256), BF16),
            pltpu.VMEM((2, 2, 3, CAP, 256), BF16),
            pltpu.VMEM((192, 512), BF16),
            pltpu.VMEM((192, 512), BF16),
            pltpu.VMEM((512, 192), BF16),
            pltpu.VMEM((2, 2, 3, 128, 256), BF16),
            pltpu.VMEM((2, 2, 3, 128, 256), BF16),
            pltpu.VMEM((2, 2, 128, 256), F32),
            pltpu.VMEM((2, 2, 128, 256), BF16),
            pltpu.VMEM((2, 2, 3, 32, 256), BF16),
            pltpu.VMEM((3, 8, 512), F32),
            pltpu.VMEM((3, 3, 8, 512), F32),
            dma((3, 4)),
            dma((4,)),
            dma((2, 2, 4, 4)),
            dma((2, 2, 4, 4)),
            dma((5, 2, 4, 2)),
            dma((5, 2, 4, 2)),
            dma((2, 3)),
            dma((2, 3)),
        ]
        + [dma((5, 3))] * 10
        + [dma((3, 3))] * 2,
        compiler_params=pltpu.CompilerParams(
            collective_id=0, has_side_effects=True, vmem_limit_bytes=40 * 1024 * 1024
        ),
    )(*[pltpu.with_memory_space_constraint(a, pltpu.HBM) for a in operands])
    return mixed, grad_tokens, grad_gates_t.T


def solution(mesh):
    return jax.shard_map(
        body,
        mesh=mesh,
        in_specs=(
            P("dp", "tensor"),
            P("dp", "tensor"),
            P("dp", None),
            P("dp", None),
            P(("expert", "tensor"), "dp", None),
            P(("expert", "tensor"), "dp", None),
            P(("expert", "tensor"), "dp", None),
        ),
        out_specs=(P("dp", "tensor"), P("dp", "tensor"), P("dp", None)),
        check_vma=False,
    )
```

time: 120 us -> 109 us (0.908)
  Pallas kernels: 115 us -> 106 us
    pallas_call x1, Pallas kernels: 115 us -> 106 us  [body(): pl.pallas_call(kernel, out_shape=(jax.ShapeDtypeStruct((512, 512), BF16),...]
    unnamed x7 -> x3, local copies, waits for them, and re-layouts: 3.33 us -> 2.19 us
where the time goes in v3:
time: 109 us
  Pallas kernels  106 us (97%)
  local copies, waits for them, and re-layouts  2.19 us (2%)
    pallas_call x1, Pallas kernels, body(): pl.pallas_call(kernel, out_shape=(jax.ShapeDtypeStruct((512, 512), BF16),...  106 us
    unnamed x3, local copies, waits for them, and re-layouts  2.19 us

profile of v3, /device:TPU:24, one launch (start us, length us, event | category | flops | bytes accessed | tf_op | source)
XLA Modules:
  0.0 108.5 jit_solution(5245093577161173733)
XLA Ops:
  0.6 105.7 %shard_map.94 = (bf16[512,512]{1,0:T(8,128)(2,1)S(1)}, bf16[512,512]{1,0:T(8,128)(2,1)S(1)}, f32[8,512]{1,0:T(8,128)S(1)}) custom-call(s32[8,512]{1,0:T(8,128)} %bitcast.4, f32[8,512]{1,0:T(8,128)} %bitcast.5, bf16[512,512]{1,0:T(8,128)(2,1)} %tok_hbm.1, bf16[512,512]{1,0:T(8,128)(2,1)} %grad_hbm.1, bf16[1,192,2048]{2,1,0:T(8,128)(2,1)} %wg_hbm.1, ...), custom_call_target="tpu_custom_call" | custom-call | tf_op jit(solution)/shard_map/pallas_call | solution.py:420
  106.4 0.8 copy.13
  107.1 0.8 copy.14
  107.9 0.6 copy.15

commit v4 on v3

--- a/solution.py
+++ b/solution.py
@@ -13,7 +13,7 @@
 ANTI = 7
 UNITS = ((0, 0, 0, 256), (0, 1, 0, 256), (1, 0, 0, 256), (1, 1, 0, 128), (1, 1, 128, 128))
 PLAN = (
-    ("ag", 0, 0, 1), ("E", 0, 0), ("E", 1, 0), ("ag", 0, 1, 0), ("ag", 1, 0, 1), ("E", 2, 0),
+    ("wm",), ("ag", 0, 0, 1), ("E", 0, 0), ("E", 1, 0), ("ag", 0, 1, 0), ("ag", 1, 0, 1), ("E", 2, 0),
     ("ag", 1, 1, 0), ("ag", 0, 1, 1), ("E", 0, 1), ("E", 1, 1), ("ag", 0, 2, 0), ("ag", 0, 0, 2),
     ("F", 0), ("ag", 0, 0, 3), ("G", 0), ("P", 0, 0, 0), ("P", 0, 0, 1), ("P", 0, 0, 2),
     ("ag", 1, 1, 1), ("P", 0, 0, 3), ("E", 2, 1), ("E", 0, 2), ("ag", 0, 2, 1), ("E", 1, 2),
@@ -28,7 +28,7 @@
     ("ag", 1, 2, 3), ("P", 0, 3, 2), ("P", 0, 3, 3), ("free", 0), ("B", 2), ("E", 2, 3),
     ("P", 1, 2, 0), ("P", 1, 2, 1), ("free", 1), ("P", 1, 2, 2), ("P", 1, 2, 3), ("ag", 1, 3, 1),
     ("ag", 1, 3, 2), ("F", 4), ("G", 4), ("P", 0, 4, 0), ("P", 0, 4, 1), ("ag", 1, 3, 3),
-    ("P", 0, 4, 2), ("P", 0, 4, 3), ("wm",), ("first", 0), ("first", 1), ("B", 3), ("P", 1, 3, 0),
+    ("P", 0, 4, 2), ("P", 0, 4, 3), ("first", 0), ("first", 1), ("B", 3), ("P", 1, 3, 0),
     ("P", 1, 3, 1), ("short", 0, 2), ("P", 1, 3, 2), ("P", 1, 3, 3), ("E", 2, 4), ("free", 2),
     ("B", 4), ("free", 3), ("P", 1, 4, 0), ("P", 1, 4, 1), ("free", 4), ("P", 1, 4, 2),
     ("long", 0, 1), ("P", 1, 4, 3), ("first", 2), ("short", 0, 3), ("short", 2, 2), ("first", 3),
@@ -90,17 +90,18 @@
         started.append(copy)
         return copy
 
-    barrier = pltpu.get_barrier_semaphore()
-    everyone = list(ring) + list(peers[1:]) + x_peers[1:] + z_peers[1:]
-    for peer in everyone:
-        pl.semaphore_signal(barrier, inc=1, device_id=peer, device_id_type=MESH)
-
     row_loads = []
     route_loads = []
     for n, (hbm, vmem) in enumerate(((routes_hbm, routes), (gates_hbm, gates))):
         load = pltpu.make_async_copy(hbm, vmem, in_sem.at[2 + n])
         load.start()
         route_loads.append(load)
+
+    barrier = pltpu.get_barrier_semaphore()
+    everyone = list(ring) + list(peers[1:]) + x_peers[1:] + z_peers[1:]
+    for peer in everyone:
+        pl.semaphore_signal(barrier, inc=1, device_id=peer, device_id_type=MESH)
+
     for kind, hbm in enumerate((tok_hbm, grad_hbm)):
         load = pltpu.make_async_copy(hbm, rows_in.at[kind], in_sem.at[kind])
         load.start()
@@ -114,6 +115,9 @@
             load.start()
             loads[n].append(load)
 
+    rows512 = lax.broadcasted_iota(jnp.int32, (512, 512), 0)
+    cols512 = lax.broadcasted_iota(jnp.int32, (512, 512), 1)
+    before = (rows512 < cols512).astype(F32).astype(BF16)
     for load in route_loads:
         load.wait()
     ids = routes[...]
@@ -125,9 +129,6 @@
         mask = jnp.sum((ids == experts[q]).astype(F32), axis=0, keepdims=True)
         masks.append(mask)
         chosen = chosen + jnp.where(row8 == q, mask, 0.0)
-    rows512 = lax.broadcasted_iota(jnp.int32, (512, 512), 0)
-    cols512 = lax.broadcasted_iota(jnp.int32, (512, 512), 1)
-    before = (rows512 < cols512).astype(F32).astype(BF16)
     rank = dot(chosen.astype(BF16), before).astype(jnp.int32)
     slot = lax.broadcasted_iota(jnp.int32, (CAP, 512), 0)
     for q in range(4):

time: 109 us -> 108 us (level)
  no operation moved by 1% of the time
where the time goes in v4:
time: 108 us
  Pallas kernels  105 us (97%)
  local copies, waits for them, and re-layouts  2.19 us (2%)
    pallas_call x1, Pallas kernels, body(): pl.pallas_call(kernel, out_shape=(jax.ShapeDtypeStruct((512, 512), BF16),...  105 us
    unnamed x3, local copies, waits for them, and re-layouts  2.19 us

profile of v4, /device:TPU:24, one launch (start us, length us, event | category | flops | bytes accessed | tf_op | source)
XLA Modules:
  0.0 108.3 jit_solution(14545503793877422333)
XLA Ops:
  0.6 105.4 %shard_map.94 = (bf16[512,512]{1,0:T(8,128)(2,1)S(1)}, bf16[512,512]{1,0:T(8,128)(2,1)S(1)}, f32[8,512]{1,0:T(8,128)S(1)}) custom-call(s32[8,512]{1,0:T(8,128)} %bitcast.4, f32[8,512]{1,0:T(8,128)} %bitcast.5, bf16[512,512]{1,0:T(8,128)(2,1)} %tok_hbm.1, bf16[512,512]{1,0:T(8,128)(2,1)} %grad_hbm.1, bf16[1,192,2048]{2,1,0:T(8,128)(2,1)} %wg_hbm.1, ...), custom_call_target="tpu_custom_call" | custom-call | tf_op jit(solution)/shard_map/pallas_call | solution.py:421
  106.1 0.8 copy.13
  106.9 0.8 copy.14
  107.7 0.6 copy.15
